TPU v7x, 256 devices: a whole 4x4x8 slice. The times are simulated.
256 devices in a mesh: grp: 32 (over z_lo, x, core), tp: 8 (over y, z_hi).
Axes of the slice: x: 4, y: 4, z: 8 (z_hi: 2, z_lo: 4; z = z_hi * 4 + z_lo), core: 2. Of those that a mesh axis runs over, the one named last changes fastest.
Arguments:
- hidden: bfloat16 [8192, 4096], P('grp'), may hold values from -6 to 6
- norm_gain: float32 [4096], replicated, may hold values from 0.1 to 1.9
- w_query: bfloat16 [4096, 2048], P(None, 'tp'), may hold values from -0.09375 to 0.09375
- w_keyval: bfloat16 [4096, 512], P(None, 'tp'), may hold values from -0.09375 to 0.09375
- w_out: bfloat16 [2048, 4096], P('tp'), may hold values from -0.125 to 0.125
- kv_cache: bfloat16 [327680, 512], P(('grp', 'tp')), may hold values from -110 to 110, as said below
- cache_len: int32 [64], replicated, may hold values from 1 to 8192, as said below
- partner: int32 [32], replicated, may hold values from 0 to 31, as said below
Outputs:
- attn_out: bfloat16 [8192, 4096], P('grp', 'tp')
Inputs may be any that keep to these rules, and one draw needn't show every extreme that they name: `cache_len`: entry g*2 is the cached length of group g's first request, at most 8192 and equal to 8192 for some group; every other entry is at most 2048, and equal to 2048 for some group. partner[g] is g XOR m for one m of 1 to 31 that is the same for every group, so partner[partner[g]] = g. `kv_cache`: cached keys and values of earlier tokens, laid out as row_owner describes.
All inputs are finite; a program needn't handle non-finite values.
Results may differ from a plain program's by a relative error of at most 0.013.
The roundings to bfloat16 on the way count: a program that leaves them out, or rounds other values in their place, can miss the bound.
Values may be sent and summed in bfloat16 or wider, within the bound.
A program may use at most 128 MiB of HBM per device.

v0:
```python
import functools

import jax
import jax.numpy as jnp
from jax import lax
from jax.experimental import pallas as pl
from jax.experimental.pallas import tpu as pltpu
from jax.sharding import PartitionSpec as P

HD = 128
QH = 16
KVH = 2
C = 128
R = 2

THETA = 5000000.0
EPS = 1e-05
NEG = -1e30
CHUNK = 256
MESH = pl.DeviceIdType.MESH


def rotate_pairs(values, positions):
    width = values.shape[-1]
    half_width = width // 2
    frequency = THETA ** (-2.0 * jnp.arange(half_width, dtype=jnp.float32) / width)
    angles = positions.astype(jnp.float32)[:, None] * frequency[None, :]
    cosine_part = jnp.cos(angles)[:, None, :]
    sine_part = jnp.sin(angles)[:, None, :]
    first_half = values[..., :half_width]
    second_half = values[..., half_width:]
    return jnp.concatenate(
        [
            first_half * cosine_part - second_half * sine_part,
            second_half * cosine_part + first_half * sine_part,
        ],
        -1,
    )


def exchange_kernel(count, stride, modes, *refs):
    arrays = len(modes)
    ins, outs = refs[:arrays], refs[arrays : 2 * arrays]
    send_sem, recv_sem = refs[2 * arrays :]
    me = lax.axis_index("tp")
    grp = lax.axis_index("grp")
    mine = lax.rem(me // stride, count)
    base = me - mine * stride

    def member(step):
        return lax.rem(mine + step, count)

    barrier = pltpu.get_barrier_semaphore()
    for step in range(1, count):
        pl.semaphore_signal(
            barrier, inc=1, device_id=(grp, base + member(step) * stride), device_id_type=MESH
        )
    pl.semaphore_wait(barrier, count - 1)
    copies = []
    for index in range(arrays):
        for step in range(1, count):
            peer = member(step)
            source = ins[index] if modes[index] else ins[index].at[peer]
            copy = pltpu.make_async_remote_copy(
                src_ref=source,
                dst_ref=outs[index].at[mine],
                send_sem=send_sem.at[index, step],
                recv_sem=recv_sem.at[index, step],
                device_id=(grp, base + peer * stride),
                device_id_type=MESH,
            )
            copy.start()
            copies.append(copy)
        if modes[index]:
            outs[index][mine] = ins[index][...]
        else:
            outs[index][mine] = ins[index][mine]
    for copy in copies:
        copy.wait()


def tp_exchange(arrays, modes, collective_id, count=None, stride=1):
    count = lax.axis_size("tp") if count is None else count
    shapes = []
    for array, gather in zip(arrays, modes):
        block = array.shape if gather else array.shape[1:]
        shapes.append(jax.ShapeDtypeStruct((count,) + tuple(block), array.dtype))
    vmem = pl.BlockSpec(memory_space=pltpu.VMEM)
    return pl.pallas_call(
        functools.partial(exchange_kernel, count, stride, tuple(modes)),
        out_shape=tuple(shapes),
        in_specs=[vmem] * len(arrays),
        out_specs=tuple([vmem] * len(arrays)),
        scratch_shapes=[
            pltpu.SemaphoreType.DMA((len(arrays), count)),
            pltpu.SemaphoreType.DMA((len(arrays), count)),
        ],
        compiler_params=pltpu.CompilerParams(
            collective_id=collective_id, has_side_effects=True, vmem_limit_bytes=48 * 1024 * 1024
        ),
    )(*arrays)


def gather_kernel(arrays, *refs):
    ins, outs = refs[:arrays], refs[arrays : 2 * arrays]
    pair_send, pair_recv, ring_send, ring_recv, hop_send, hop_recv = refs[2 * arrays :]
    me = lax.axis_index("tp")
    grp = lax.axis_index("grp")
    ring = lax.axis_size("tp") // 2
    side = me % 2
    ring_at = me // 2
    partner = (grp, ring_at * 2 + 1 - side)

    def member(step):
        return (grp, lax.rem(ring_at + step, ring) * 2 + side)

    barrier = pltpu.get_barrier_semaphore()
    pl.semaphore_signal(barrier, inc=1, device_id=partner, device_id_type=MESH)
    for step in range(1, ring):
        pl.semaphore_signal(barrier, inc=1, device_id=member(step), device_id_type=MESH)
    pl.semaphore_wait(barrier, ring)
    pairs, direct = [], []
    for index in range(arrays):
        copy = pltpu.make_async_remote_copy(
            src_ref=ins[index],
            dst_ref=outs[index].at[ring_at, side],
            send_sem=pair_send.at[index],
            recv_sem=pair_recv.at[index],
            device_id=partner,
            device_id_type=MESH,
        )
        copy.start()
        pairs.append(copy)
        for step in range(1, ring):
            copy = pltpu.make_async_remote_copy(
                src_ref=ins[index],
                dst_ref=outs[index].at[ring_at, side],
                send_sem=ring_send.at[index, step],
                recv_sem=ring_recv.at[index, step],
                device_id=member(step),
                device_id_type=MESH,
            )
            copy.start()
            direct.append(copy)
        outs[index][ring_at, side] = ins[index][...]
    hops = []
    for index in range(arrays):
        pairs[index].wait_recv()
        for step in range(1, ring):
            copy = pltpu.make_async_remote_copy(
                src_ref=outs[index].at[ring_at, 1 - side],
                dst_ref=outs[index].at[ring_at, 1 - side],
                send_sem=hop_send.at[index, step],
                recv_sem=hop_recv.at[index, step],
                device_id=member(step),
                device_id_type=MESH,
            )
            copy.start()
            hops.append(copy)
    for copy in pairs:
        copy.wait_send()
    for copy in direct + hops:
        copy.wait()


def group_gather(arrays, collective_id):
    ring = lax.axis_size("tp") // 2
    count = len(arrays)
    shapes = [jax.ShapeDtypeStruct((ring, 2) + a.shape, a.dtype) for a in arrays]
    vmem = pl.BlockSpec(memory_space=pltpu.VMEM)
    return pl.pallas_call(
        functools.partial(gather_kernel, count),
        out_shape=tuple(shapes),
        in_specs=[vmem] * count,
        out_specs=tuple([vmem] * count),
        scratch_shapes=[
            pltpu.SemaphoreType.DMA((count,)),
            pltpu.SemaphoreType.DMA((count,)),
            pltpu.SemaphoreType.DMA((count, ring)),
            pltpu.SemaphoreType.DMA((count, ring)),
            pltpu.SemaphoreType.DMA((count, ring)),
            pltpu.SemaphoreType.DMA((count, ring)),
        ],
        compiler_params=pltpu.CompilerParams(
            collective_id=collective_id, has_side_effects=True, vmem_limit_bytes=48 * 1024 * 1024
        ),
    )(*arrays)


def attention_kernel(lo_ref, hi_ref, q_ref, cache_ref, mix_ref, peak_ref, total_ref):
    block = pl.program_id(0)
    kv_head = pl.program_id(1)
    lo = lo_ref[block]
    hi = hi_ref[block]
    heads, tokens, width = q_ref.shape
    key_col = pl.multiple_of(kv_head * HD, HD)
    value_col = pl.multiple_of((KVH + kv_head) * HD, HD)
    first = lo // CHUNK
    last = jnp.where(hi > lo, (hi + CHUNK - 1) // CHUNK, first)

    def one_head(head, carry):
        query = q_ref[head]

        def body(chunk, state):
            peak, total, mix = state
            start = pl.multiple_of(chunk * CHUNK, CHUNK)
            keys = cache_ref[pl.ds(start, CHUNK), pl.ds(key_col, HD)]
            values = cache_ref[pl.ds(start, CHUNK), pl.ds(value_col, HD)]
            rows = start + lax.broadcasted_iota(jnp.int32, (1, CHUNK), 1)
            bias = jnp.where((rows >= lo) & (rows < hi), 0.0, -jnp.inf)
            scores = lax.dot_general(
                query, keys, (((1,), (1,)), ((), ())), preferred_element_type=jnp.float32
            ) * (HD ** (-0.5)) + bias
            new_peak = jnp.maximum(peak, jnp.max(scores, axis=1, keepdims=True))
            scale = jnp.exp(peak - new_peak)
            weights = jnp.exp(scores - new_peak)
            total = scale * total + jnp.sum(weights, axis=1, keepdims=True)
            mix = scale * mix + jnp.dot(
                weights.astype(jnp.bfloat16), values, preferred_element_type=jnp.float32
            )
            return new_peak, total, mix

        start_state = (
            jnp.full((tokens, 1), NEG, jnp.float32),
            jnp.zeros((tokens, 1), jnp.float32),
            jnp.zeros((tokens, width), jnp.float32),
        )
        peak, total, mix = lax.fori_loop(first, last, body, start_state)
        mix_ref[head] = mix
        peak_ref[head] = peak
        total_ref[head] = total
        return carry

    lax.fori_loop(0, heads, one_head, 0)


def cache_attention(queries, cache_rows, lo, hi):
    heads, tokens, width = queries.shape
    blocks = tokens // C
    group_size = heads // KVH
    return pl.pallas_call(
        attention_kernel,
        out_shape=(
            jax.ShapeDtypeStruct((heads, tokens, width), jnp.float32),
            jax.ShapeDtypeStruct((heads, tokens, 1), jnp.float32),
            jax.ShapeDtypeStruct((heads, tokens, 1), jnp.float32),
        ),
        grid_spec=pltpu.PrefetchScalarGridSpec(
            num_scalar_prefetch=2,
            grid=(blocks, KVH),
            in_specs=[
                pl.BlockSpec((group_size, C, width), lambda b, j, lo, hi: (j, b, 0)),
                pl.BlockSpec(cache_rows.shape, lambda b, j, lo, hi: (0, 0)),
            ],
            out_specs=[
                pl.BlockSpec((group_size, C, width), lambda b, j, lo, hi: (j, b, 0)),
                pl.BlockSpec((group_size, C, 1), lambda b, j, lo, hi: (j, b, 0)),
                pl.BlockSpec((group_size, C, 1), lambda b, j, lo, hi: (j, b, 0)),
            ],
        ),
        compiler_params=pltpu.CompilerParams(vmem_limit_bytes=48 * 1024 * 1024),
    )(lo, hi, queries, cache_rows)


def join_partials(first, second):
    first_mix, first_peak, first_total = first
    second_mix, second_peak, second_total = second
    new_peak = jnp.maximum(first_peak, second_peak)
    first_scale = jnp.exp(first_peak - new_peak)
    second_scale = jnp.exp(second_peak - new_peak)
    joined_mix = first_mix * first_scale[..., None] + second_mix * second_scale[..., None]
    return (joined_mix, new_peak, first_total * first_scale + second_total * second_scale)


def to_partner(tree, flip_mask, groups):
    def branch(mask):
        pairs = [(i, i ^ mask) for i in range(groups)]
        return lambda t: jax.tree.map(lambda a: lax.ppermute(a, "grp", pairs), t)

    low_count = 8
    low = lax.rem(flip_mask, low_count)
    high = flip_mask // low_count
    tree = lax.switch(low, [lambda t: t] + [branch(mask) for mask in range(1, low_count)], tree)
    high_masks = range(low_count, groups, low_count)
    return lax.switch(high, [lambda t: t] + [branch(mask) for mask in high_masks], tree)


def on_device(hidden, norm_gain, w_query, w_keyval, w_out, kv_cache, cache_len, partner):
    group_index = lax.axis_index("grp")
    tp_index = lax.axis_index("tp")
    tp_count = lax.axis_size("tp")
    groups = lax.axis_size("grp")
    ring = tp_count // 2
    ring_at = tp_index // 2
    side = tp_index % 2
    local_heads = QH // tp_count
    rows_here = kv_cache.shape[0]
    token_count = hidden.shape[0]
    model_width = w_out.shape[1]
    out_width = model_width // tp_count
    flip_mask = partner[0]

    def w_block(member):
        first = lax.dynamic_slice_in_dim(w_out, (2 * member + side) * out_width, out_width, 1)
        second = lax.dynamic_slice_in_dim(w_out, (2 * member + 1 - side) * out_width, out_width, 1)
        return jnp.concatenate([first, second], 1)

    w_received = [w_block(ring_at)]
    for step in range(1, ring):
        send = w_block(lax.rem(ring_at + step, ring))
        pairs = [(i, (i + 2 * step) % tp_count) for i in range(tp_count)]
        w_received.append(lax.ppermute(send, "tp", pairs))

    float_rows = hidden.astype(jnp.float32)
    normed = (
        float_rows
        * lax.rsqrt(jnp.mean(float_rows * float_rows, -1, keepdims=True) + EPS)
        * norm_gain
    ).astype(jnp.bfloat16)
    query_raw = jnp.dot(normed, w_query, preferred_element_type=jnp.float32).reshape(
        token_count, local_heads, HD
    )
    keyval_part = jnp.dot(normed, w_keyval, preferred_element_type=jnp.float32).astype(jnp.bfloat16)
    lengths = lax.dynamic_slice_in_dim(cache_len, group_index * R, R)
    positions = (lengths[:, None] + jnp.arange(C, dtype=jnp.int32)[None, :]).reshape(token_count)
    query_local = rotate_pairs(query_raw, positions).astype(jnp.bfloat16).transpose(1, 0, 2)
    far_query = to_partner(query_local[:, :C], flip_mask, groups)
    query_ext = jnp.concatenate([query_local, far_query], 1)
    ext_tokens = query_ext.shape[1]
    query_got, keyval_got = group_gather([query_ext, keyval_part], 0)
    queries = query_got.reshape(QH, ext_tokens, HD)
    keyval_all = keyval_got.reshape(tp_count, token_count, -1).transpose(1, 0, 2).reshape(
        token_count, -1
    )

    stored_first = lengths[0] - lengths[0] // 2
    bound_one = stored_first
    bound_two = stored_first + lengths[1]
    far_count = cache_len[partner[group_index] * R] // 2
    starts = jnp.stack([0, bound_one, bound_two]).astype(jnp.int32)
    ends = jnp.stack([bound_one, bound_two, bound_two + far_count]).astype(jnp.int32)
    offset = tp_index * rows_here
    lo = jnp.clip(starts - offset, 0, rows_here)
    hi = jnp.clip(ends - offset, 0, rows_here)
    mix, peak, total = cache_attention(queries, kv_cache, lo, hi)
    mix_got, peak_got, total_got = tp_exchange(
        [
            mix.astype(jnp.bfloat16).reshape(tp_count, local_heads, ext_tokens, HD),
            peak.reshape(tp_count, local_heads, ext_tokens),
            total.reshape(tp_count, local_heads, ext_tokens),
        ],
        [False, False, False],
        2,
    )
    top = jnp.max(peak_got, 0)
    scales = jnp.exp(peak_got - top[None])
    mix_c = jnp.sum(mix_got.astype(jnp.float32) * scales[..., None], 0)
    total_c = jnp.sum(total_got * scales, 0)
    far_pack = jnp.concatenate(
        [
            mix_c[:, token_count:],
            top[:, None, token_count:],
            total_c[:, None, token_count:],
        ],
        1,
    )
    far_pack = to_partner(far_pack, flip_mask, groups)
    far_back = (far_pack[:, :C], far_pack[:, C], far_pack[:, C + 1])
    combined = (mix_c[:, :token_count], top[:, :token_count], total_c[:, :token_count])
    front = join_partials(tuple(piece[:, :C] for piece in combined), far_back)
    own = tuple(jnp.concatenate([front[i], combined[i][:, C:]], 1) for i in range(3))

    new_keys = rotate_pairs(
        keyval_all[:, : KVH * HD].astype(jnp.float32).reshape(token_count, KVH, HD), positions
    ).astype(jnp.bfloat16)
    new_values = keyval_all[:, KVH * HD :].reshape(token_count, KVH, HD)
    kv_head = (tp_index * local_heads) // (QH // KVH)
    key_rows = lax.dynamic_index_in_dim(new_keys, kv_head, 1, keepdims=False)
    value_rows = lax.dynamic_index_in_dim(new_values, kv_head, 1, keepdims=False)
    token_index = jnp.arange(token_count, dtype=jnp.int32)
    request_of = token_index // C
    within = token_index % C
    self_visible = (request_of[:, None] == request_of[None, :]) & (
        within[None, :] <= within[:, None]
    )
    self_scores = jnp.einsum(
        "htd,sd->hts", query_local, key_rows, preferred_element_type=jnp.float32
    ) * HD ** (-0.5)
    self_scores = jnp.where(self_visible[None], self_scores, -jnp.inf)
    self_peak = jnp.max(self_scores, -1)
    self_weights = jnp.exp(self_scores - self_peak[..., None])
    self_total = jnp.sum(self_weights, -1)
    self_mix = jnp.einsum(
        "hts,sd->htd", self_weights.astype(jnp.bfloat16), value_rows,
        preferred_element_type=jnp.float32,
    )
    final_mix, final_peak, final_total = join_partials(own, (self_mix, self_peak, self_total))
    attention = (final_mix / final_total[..., None]).astype(jnp.bfloat16)
    attention = attention.transpose(1, 0, 2).reshape(token_count, local_heads * HD)
    (attention_ring,) = tp_exchange([attention], [True], 3, ring, 2)
    sums = None
    for step in range(ring):
        source = lax.rem(ring_at - step + ring, ring)
        piece = jnp.dot(
            lax.dynamic_index_in_dim(attention_ring, source, 0, False),
            w_received[step],
            preferred_element_type=jnp.float32,
        )
        sums = piece if sums is None else sums + piece
    (other_got,) = tp_exchange([sums[:, out_width:].astype(jnp.bfloat16)], [True], 4, 2, 1)
    other = lax.dynamic_index_in_dim(other_got, 1 - side, 0, False)
    return (sums[:, :out_width] + other.astype(jnp.float32)).astype(jnp.bfloat16)


def solution(mesh):
    placed = (
        P("grp", None),
        P(),
        P(None, "tp"),
        P(None, "tp"),
        P("tp", None),
        P(("grp", "tp"), None),
        P(),
        P(),
    )
    return jax.shard_map(
        on_device, mesh=mesh, in_specs=placed, out_specs=P("grp", "tp"), check_vma=False
    )
```

profile of v0, /device:TPU:4, one launch (start us, length us, event | category | flops | bytes accessed | tf_op | source)
XLA Modules:
  0.0 225.4 jit_solution(9308923703706514268)
XLA Ops:
  0.0 2.6 %constant_dynamic-slice_fusion.3 = (bf16[256,512]{1,0:T(8,128)(2,1)S(1)}, bf16[256,512]{1,0:T(8,128)(2,1)S(1)}, bf16[256,512]{1,0:T(8,128)(2,1)S(1)}, bf16[256,5...) fusion(bf16[256,4096]{1,0:T(8,128)(2,1)} %param.36, ...), kind=kLoop, calls=%fused_computation.64 | loop fusion | bytes 4194336 | tf_op jit(solution)/shard_map/dynamic_slice | solution.py:304
  3.5 1.6 collective-permute-start.20
  5.9 1.7 collective-permute-start.22
  8.5 2.0 collective-permute-start.21
  21.1 2.2 fusion
  26.2 4.4 %conditional.4 = (bf16[2,128,128]{2,1,0:T(8,128)(2,1)S(1)}) conditional(s32[]{:T(128)} %clamp.11, bf16[2,128,128]{2,1,0:T(8,128)(2,1)S(1)} %slice.133, bf16[2,128,128]{2,1,0:T(8,128)(2,1)S(1)} %slice.133, bf16[2,128,128]{2,1,0:T(8,128)(2,1)S(1)} %slice.133, bf16[2,128,128]{2,1,0:T(8,128)(2,1)S(1)} %slice.133, ...), branch_computations={%region_1.2_spmd, %region_2.3_spmd, %region_3.4_spmd, %region_4.5_... | conditional | bytes 393264 | solution.py:283
  26.3 1.3 collective-permute-start.1
  27.5 3.1 %collective-permute-done.1 = bf16[2,128,128]{2,1,0:T(8,128)(2,1)S(1)} collective-permute-done((bf16[2,128,128]{2,1,0:T(8,128)(2,1)S(1)}, bf16[2,128,128]{2,1,0:T(8,128)(2,1)S(1)}, u32[]{:S(2)}, u32[]{:S(2)}) %collective-permute-start.1) | collective-permute-done | bytes 65568 | tf_op jit(solution)/shard_map/cond/branch_2_fun/ppermute | solution.py:278
  30.6 5.5 %conditional.5 = (bf16[2,128,128]{2,1,0:T(8,128)(2,1)S(1)}) conditional(s32[]{:T(128)} %clamp.10, bf16[2,128,128]{2,1,0:T(8,128)(2,1)S(1)} %get-tuple-element.120, bf16[2,128,128]{2,1,0:T(8,128)(2,1)S(1)} %get-tuple-element.120, bf16[2,128,128]{2,1,0:T(8,128)(2,1)S(1)} %get-tuple-element.120, ...), branch_computations={%region_9.10_spmd, %region_10.11_spmd, %region_11.12_spmd, %region... | conditional | bytes 393264 | solution.py:285
  30.6 3.3 %collective-permute-start.8 = (bf16[2,128,128]{2,1,0:T(8,128)(2,1)S(1)}, bf16[2,128,128]{2,1,0:T(8,128)(2,1)S(1)}, u32[]{:S(2)}, u32[]{:S(2)}) collective-permute-start(bf16[2,128,128]{2,1,0:T(8,128)(2,1)S(1)} %param.10), channel_id=1, source_target_pairs={{0,128},{8,136},{16,144},{24,152},{32,160},{40,168},{48,176},{56,1... | collective-permute-start | bytes 196616 | tf_op jit(solution)/shard_map/cond/branch_2_fun/ppermute | solution.py:278
  33.9 2.2 collective-permute-done.8
  36.8 2.6 %convolution_convert_fusion = bf16[256,64]{0,1:T(8,128)(2,1)S(1)} fusion(bf16[4096,64]{0,1:T(8,128)(2,1)} %param.35, bf16[256,4096]{1,0:T(8,128)(2,1)} %param.32, f32[4096]{0:T(1024)S(1)} %copy-done.23, f32[256]{0:T(256)S(1)} %add_rsqrt_fusion), kind=kOutput, calls=%fused_computation.15 | convolution fusion | flops 138428416 | bytes 2671616 | tf_op jit(solution)/shard_map/dot_general | solution.py:323
  41.2 29.7 %shard_map.82 = (bf16[4,2,2,384,128]{4,3,2,1,0:T(8,128)(2,1)S(1)}, bf16[4,2,256,64]{3,2,1,0:T(8,128)(2,1)S(1)}) custom-call(bf16[2,384,128]{2,1,0:T(8,128)(2,1)S(1)} %copy-done.6, bf16[256,64]{1,0:T(8,128)(2,1)S(1)} %copy.80.refs_1_), custom_call_target="tpu_custom_call" | custom-call | tf_op jit(solution)/shard_map/pallas_call | solution.py:171
  73.7 1.4 copy-done.3
  75.1 47.9 %shard_map.83 = (f32[16,384,128]{2,1,0:T(8,128)S(1)}, f32[16,384,1]{2,1,0:T(8,128)}, f32[16,384,1]{2,1,0:T(8,128)}) custom-call(s32[3]{0:T(128)S(1)} %get-tuple-element.118.lo_ref, s32[3]{0:T(128)S(1)} %get-tuple-element.119.hi_ref, bf16[16,384,128]{2,1,0:T(8,128)(2,1)S(1)} %bitcast.67, bf16[1280,512]{1,0:T(8,128)(2,1)S(1)} %copy-done.5), custom_call_target="tpu_custom_call" | custom-call | tf_op jit(solution)/shard_map/pallas_call | solution.py:241
  123.0 1.5 convert_element_type.50
  124.5 2.8 %reduce = f32[16,384]{1,0:T(8,128)S(1)} reduce(f32[16,384,1]{2,1,0:T(8,128)} %get-tuple-element.67, f32[]{:T(128)} %constant.178), dimensions={2}, to_apply=%get-tuple-element.67.reduce_sub_computation | reduce | bytes 49156 | tf_op jit(solution)/shard_map/pallas_call | solution.py:241
  127.3 2.8 %reduce.1 = f32[16,384]{1,0:T(8,128)S(1)} reduce(f32[16,384,1]{2,1,0:T(8,128)} %get-tuple-element.68, f32[]{:T(128)} %constant.178), dimensions={2}, to_apply=%get-tuple-element.68.reduce_sub_computation | reduce | bytes 49156 | tf_op jit(solution)/shard_map/pallas_call | solution.py:241
  130.1 1.4 copy-done.1
  131.5 40.4 %shard_map.84 = (bf16[8,2,384,128]{3,2,1,0:T(8,128)(2,1)S(1)}, f32[8,2,384]{2,1,0:T(2,128)S(1)}, f32[8,2,384]{2,1,0:T(2,128)S(1)}) custom-call(bf16[8,2,384,128]{3,2,1,0:T(8,128)(2,1)S(1)} %bitcast.66, f32[8,2,384]{2,1,0:T(2,128)S(1)} %reshape.299.refs_1_, f32[8,2,384]{2,1,0:T(2,128)S(1)} %reshape.300.refs_2_), custom_call_target="tpu_custom_call" | custom-call | tf_op jit(solution)/shard_map/pallas_call | solution.py:89
  173.7 2.1 multiply_reduce_fusion
  176.6 5.5 %conditional.6 = (f32[2,130,128]{2,1,0:T(8,128)S(1)}) conditional(s32[]{:T(128)} %clamp.11, f32[2,130,128]{2,1,0:T(8,128)S(1)} %pad_maximum_fusion.4, f32[2,130,128]{2,1,0:T(8,128)S(1)} %pad_maximum_fusion.4, f32[2,130,128]{2,1,0:T(8,128)S(1)} %pad_maximum_fusion.4, ...), branch_computations={%region_16.17_spmd, %region_17.18_spmd, %region_18.19_spmd, %regio... | conditional | bytes 798768 | solution.py:283
  176.7 5.3 %collective-permute-done.11 = f32[2,130,128]{2,1,0:T(8,128)S(1)} collective-permute-done((f32[2,130,128]{2,1,0:T(8,128)S(1)}, f32[2,130,128]{2,1,0:T(8,128)S(1)}, u32[]{:S(2)}, u32[]{:S(2)}) %collective-permute-start.11) | collective-permute-done | bytes 133152 | tf_op jit(solution)/shard_map/cond/branch_2_fun/ppermute | solution.py:278
  182.1 6.3 %conditional.7 = (f32[2,130,128]{2,1,0:T(8,128)S(1)}) conditional(s32[]{:T(128)} %clamp.10, f32[2,130,128]{2,1,0:T(8,128)S(1)} %get-tuple-element.122, f32[2,130,128]{2,1,0:T(8,128)S(1)} %get-tuple-element.122, f32[2,130,128]{2,1,0:T(8,128)S(1)} %get-tuple-element.122, f32[2,130,128]{2,1,0:T(8,128)S(1)} %get-tuple-element.122), branch_computations={%region_24.25_spmd, %region_25.26_spmd, %region_26.27_spmd, %regio... | conditional | bytes 798768 | solution.py:285
  182.2 5.9 %collective-permute-done.18 = f32[2,130,128]{2,1,0:T(8,128)S(1)} collective-permute-done((f32[2,130,128]{2,1,0:T(8,128)S(1)}, f32[2,130,128]{2,1,0:T(8,128)S(1)}, u32[]{:S(2)}, u32[]{:S(2)}) %collective-permute-start.18) | collective-permute-done | bytes 133152 | tf_op jit(solution)/shard_map/cond/branch_2_fun/ppermute | solution.py:278
  191.3 1.6 copy.99
  194.5 1.2 fusion.60
  197.9 8.1 %shard_map.85 = bf16[4,256,256]{2,1,0:T(8,128)(2,1)S(1)} custom-call(bf16[256,256]{1,0:T(8,128)(2,1)S(1)} %copy.93.refs_0_), custom_call_target="tpu_custom_call" | custom-call | tf_op jit(solution)/shard_map/pallas_call | solution.py:89
  206.4 1.3 fusion.20
  207.8 1.3 convolution_add_fusion.1
  209.1 1.4 fusion.3
  210.5 14.1 %shard_map.86 = bf16[2,256,512]{2,1,0:T(8,128)(2,1)S(1)} custom-call(bf16[256,512]{1,0:T(8,128)(2,1)S(1)} %slice.161.refs_0_), custom_call_target="tpu_custom_call" | custom-call | tf_op jit(solution)/shard_map/pallas_call | solution.py:89
  (107 shorter events, 21.8 us)
Async XLA Ops:
  0.0 23.4 %copy-start = (bf16[4096,256]{1,0:T(8,128)(2,1)S(1)}, bf16[4096,256]{1,0:T(8,128)(2,1)}, u32[]{:S(2)}) copy-start(bf16[4096,256]{1,0:T(8,128)(2,1)} %param.34) | copy-start | bytes 6291460
  2.6 7.9 %copy-start.22 = (s32[32]{0:T(128)S(1)}, s32[32]{0:T(128)}, u32[]{:S(2)}) copy-start(s32[32]{0:T(128)} %param.39) | copy-start | bytes 388
  2.6 11.7 %copy-start.24 = (s32[64]{0:T(128)S(1)}, s32[64]{0:T(128)}, u32[]{:S(2)}) copy-start(s32[64]{0:T(128)} %param.38) | copy-start | bytes 772
  3.5 204.3 %collective-permute-start.20 = (bf16[256,1024]{1,0:T(8,128)(2,1)}, bf16[256,1024]{1,0:T(8,128)(2,1)}, u32[]{:S(2)}, u32[]{:S(2)}) collective-permute-start(bf16[256,1024]{1,0:T(8,128)(2,1)} %pad_maximum_fusion), channel_id=1, source_target_pairs={{0,2},{1,3},{2,4},{3,5},{4,6},{5,7},{6,0},{7,1},{8,10},{9,11},{10,... | collective-permute-start | bytes 1572872 | tf_op jit(solution)/shard_map/ppermute | solution.py:312
  5.1 18.3 %copy-start.23 = (f32[4096]{0:T(1024)S(1)}, f32[4096]{0:T(1024)}, u32[]{:S(2)}) copy-start(f32[4096]{0:T(1024)} %param.33) | copy-start | bytes 49156
  5.9 200.5 %collective-permute-start.22 = (bf16[256,1024]{1,0:T(8,128)(2,1)}, bf16[256,1024]{1,0:T(8,128)(2,1)}, u32[]{:S(2)}, u32[]{:S(2)}) collective-permute-start(bf16[256,1024]{1,0:T(8,128)(2,1)} %pad_maximum_fusion.2), channel_id=1, source_target_pairs={{0,6},{1,7},{2,0},{3,1},{4,2},{5,3},{6,4},{7,5},{8,14},{9,15},{10,... | collective-permute-start | bytes 1572872 | tf_op jit(solution)/shard_map/ppermute | solution.py:312
  8.5 200.7 %collective-permute-start.21 = (bf16[256,1024]{1,0:T(8,128)(2,1)}, bf16[256,1024]{1,0:T(8,128)(2,1)}, u32[]{:S(2)}, u32[]{:S(2)}) collective-permute-start(bf16[256,1024]{1,0:T(8,128)(2,1)} %pad_maximum_fusion.1), channel_id=1, source_target_pairs={{0,4},{1,5},{2,6},{3,7},{4,0},{5,1},{6,2},{7,3},{8,12},{9,13},{10,... | collective-permute-start | bytes 1572872 | tf_op jit(solution)/shard_map/ppermute | solution.py:312
  21.1 2.3 %copy-start.9 = (bf16[256,4096]{1,0:T(8,128)(2,1)S(1)}, bf16[256,4096]{1,0:T(8,128)(2,1)}, u32[]{:S(2)}) copy-start(bf16[256,4096]{1,0:T(8,128)(2,1)} %param.32) | copy-start | bytes 6291460
  25.4 0.7 copy-start.12
  25.4 0.7 copy-start.14
  26.2 9.9 %copy-start.10 = (bf16[2,256,128]{2,1,0:T(8,128)(2,1)}, bf16[2,256,128]{2,1,0:T(8,128)(2,1)S(1)}, u32[]{:S(2)}) copy-start(bf16[2,256,128]{2,1,0:T(8,128)(2,1)S(1)} %maximum_bitcast_fusion) | copy-start | bytes 393220
  26.3 4.4 %collective-permute-start.1 = (bf16[2,128,128]{2,1,0:T(8,128)(2,1)S(1)}, bf16[2,128,128]{2,1,0:T(8,128)(2,1)S(1)}, u32[]{:S(2)}, u32[]{:S(2)}) collective-permute-start(bf16[2,128,128]{2,1,0:T(8,128)(2,1)S(1)} %param.2), channel_id=1, source_target_pairs={{0,16},{8,24},{16,0},{24,8},{32,48},{40,56},{48,32},{56,40},{64,80... | collective-permute-start | bytes 196616 | tf_op jit(solution)/shard_map/cond/branch_2_fun/ppermute | solution.py:278
  30.6 5.5 %collective-permute-start.8 = (bf16[2,128,128]{2,1,0:T(8,128)(2,1)S(1)}, bf16[2,128,128]{2,1,0:T(8,128)(2,1)S(1)}, u32[]{:S(2)}, u32[]{:S(2)}) collective-permute-start(bf16[2,128,128]{2,1,0:T(8,128)(2,1)S(1)} %param.10), channel_id=1, source_target_pairs={{0,128},{8,136},{16,144},{24,152},{32,160},{40,168},{48,176},{56,1... | collective-permute-start | bytes 196616 | tf_op jit(solution)/shard_map/cond/branch_2_fun/ppermute | solution.py:278
  36.8 36.9 %copy-start.5 = (bf16[1280,512]{1,0:T(8,128)(2,1)S(1)}, bf16[1280,512]{1,0:T(8,128)(2,1)}, u32[]{:S(2)}) copy-start(bf16[1280,512]{1,0:T(8,128)(2,1)} %cache_ref.1) | copy-start | bytes 3932164
  40.3 0.9 copy-start.6
  70.9 1.2 copy-start.2
  72.1 0.8 copy-start.7
  73.7 1.4 copy-start.3
  130.1 1.4 copy-start.1
  171.9 1.2 copy-start.4
  175.9 13.2 %copy-start.8 = (bf16[4,2,256,64]{3,2,1,0:T(8,128)(2,1)S(1)}, bf16[4,2,256,64]{3,2,1,0:T(8,128)(2,1)}, u32[]{:S(2)}) copy-start(bf16[4,2,256,64]{3,2,1,0:T(8,128)(2,1)} %copy-done.7) | copy-start | bytes 786436
  176.6 5.4 %collective-permute-start.11 = (f32[2,130,128]{2,1,0:T(8,128)S(1)}, f32[2,130,128]{2,1,0:T(8,128)S(1)}, u32[]{:S(2)}, u32[]{:S(2)}) collective-permute-start(f32[2,130,128]{2,1,0:T(8,128)S(1)} %param.14), channel_id=1, source_target_pairs={{0,16},{8,24},{16,0},{24,8},{32,48},{40,56},{48,32},{56,40},{64,80... | collective-permute-start | bytes 399368 | tf_op jit(solution)/shard_map/cond/branch_2_fun/ppermute | solution.py:278
  182.1 11.5 %copy-start.13 = (f32[256,64]{1,0:T(8,128)S(1)}, f32[256,64]{1,0:T(8,128)}, u32[]{:S(2)}) copy-start(f32[256,64]{1,0:T(8,128)} %copy-done.12) | copy-start | bytes 196612
  182.1 11.5 %copy-start.15 = (f32[256,64]{1,0:T(8,128)S(1)}, f32[256,64]{1,0:T(8,128)}, u32[]{:S(2)}) copy-start(f32[256,64]{1,0:T(8,128)} %copy-done.14) | copy-start | bytes 196612
  182.1 6.0 %collective-permute-start.18 = (f32[2,130,128]{2,1,0:T(8,128)S(1)}, f32[2,130,128]{2,1,0:T(8,128)S(1)}, u32[]{:S(2)}, u32[]{:S(2)}) collective-permute-start(f32[2,130,128]{2,1,0:T(8,128)S(1)} %param.22), channel_id=1, source_target_pairs={{0,128},{8,136},{16,144},{24,152},{32,160},{40,168},{48,176},{56,1... | collective-permute-start | bytes 399368 | tf_op jit(solution)/shard_map/cond/branch_2_fun/ppermute | solution.py:278
  189.0 5.5 %copy-start.11 = (bf16[2,256,128]{2,1,0:T(8,128)(2,1)S(1)}, bf16[2,256,128]{2,1,0:T(8,128)(2,1)}, u32[]{:S(2)}) copy-start(bf16[2,256,128]{2,1,0:T(8,128)(2,1)} %copy-done.10) | copy-start | bytes 393220
  189.9 3.0 %copy-start.20 = (f32[2,1,128]{2,1,0:T(1,128)S(1)}, f32[2,1,128]{2,1,0:T(1,128)}, u32[]{:S(2)}) copy-start(f32[2,1,128]{2,1,0:T(1,128)} %get-tuple-element.101) | copy-start | bytes 3076
  189.9 3.0 %copy-start.21 = (f32[2,1,128]{2,1,0:T(1,128)S(1)}, f32[2,1,128]{2,1,0:T(1,128)}, u32[]{:S(2)}) copy-start(f32[2,1,128]{2,1,0:T(1,128)} %get-tuple-element.102) | copy-start | bytes 3076
  193.6 2.3 %copy-start.18 = (f32[2,128]{1,0:T(2,128)S(1)}, f32[2,128]{1,0:T(2,128)}, u32[]{:S(2)}) copy-start(f32[2,128]{1,0:T(2,128)} %get-tuple-element.77) | copy-start | bytes 3076
  193.6 2.3 %copy-start.19 = (f32[2,128]{1,0:T(2,128)S(1)}, f32[2,128]{1,0:T(2,128)}, u32[]{:S(2)}) copy-start(f32[2,128]{1,0:T(2,128)} %get-tuple-element.78) | copy-start | bytes 3076
  194.5 11.6 %copy-start.16 = (bf16[256,512]{1,0:T(8,128)(2,1)S(1)}, bf16[256,512]{1,0:T(8,128)(2,1)}, u32[]{:S(2)}) copy-start(bf16[256,512]{1,0:T(8,128)(2,1)} %get-tuple-element.86) | copy-start | bytes 786436
  194.5 11.6 %copy-start.17 = (bf16[256,512]{1,0:T(8,128)(2,1)S(1)}, bf16[256,512]{1,0:T(8,128)(2,1)}, u32[]{:S(2)}) copy-start(bf16[256,512]{1,0:T(8,128)(2,1)} %get-tuple-element.87) | copy-start | bytes 786436
where the time goes:
time: 226 us; the launch traced here: 225 us
  Pallas kernels  140 us (62%)
  other arithmetic  18.8 us (8%)
  local copies, waits for them, and re-layouts  18.6 us (8%)
  waiting for transfers between devices  16.6 us (7%)
  matrix products  10.5 us (5%)
  between operations  10.5 us (5%)
  starting transfers between devices  9.96 us (4%)
    pallas_call x3, Pallas kernels, tp_exchange(): pl.pallas_call(functools.partial(exchange_kernel, count, stride, tuple(mo...  62.6 us
    pallas_call x1, Pallas kernels, cache_attention(): pl.pallas_call(attention_kernel, out_shape=(jax.ShapeDtypeStruct((heads,...  47.9 us
    pallas_call x1, Pallas kernels, group_gather(): pl.pallas_call(functools.partial(gather_kernel, count), out_shape=tuple(s...  29.7 us
    ppermute x4, waiting for transfers between devices, branch(): return lambda t: jax.tree.map(lambda a: lax.ppermute(a, 'grp', pairs), t)  16.5 us
    unnamed x57, local copies, waits for them, and re-layouts  10.8 us
    pallas_call x2, other arithmetic, cache_attention(): pl.pallas_call(attention_kernel, out_shape=(jax.ShapeDtypeStruct((heads,...  5.54 us
    ppermute x3, starting transfers between devices, on_device(): w_received.append(lax.ppermute(send, 'tp', pairs))  5.22 us
    ppermute x4, starting transfers between devices, branch(): return lambda t: jax.tree.map(lambda a: lax.ppermute(a, 'grp', pairs), t)  4.74 us
  transfers between devices with their start and end apart: 7, of which 4 were waited for; matrix products, arithmetic and copies ran while one was open for 15% of the time, Pallas kernels for 56%

commit v1 on v0

--- a/solution.py
+++ b/solution.py
@@ -16,7 +16,7 @@
 THETA = 5000000.0
 EPS = 1e-05
 NEG = -1e30
-CHUNK = 256
+CHUNK = 128
 MESH = pl.DeviceIdType.MESH
 
 

time: 226 us -> 255 us (1.13)
  Pallas kernels: 140 us -> 168 us
    pallas_call x1, Pallas kernels: 47.9 us -> 64.1 us  [cache_attention(): pl.pallas_call(attention_kernel, out_shape=(jax.ShapeDtypeStruct((heads,...]
    pallas_call x3, Pallas kernels: 62.6 us -> 74.6 us  [tp_exchange(): pl.pallas_call(functools.partial(exchange_kernel, count, stride, tuple(mo...]
  transfers between devices with their start and end apart: 7 -> 7, of which waited for: 4 -> 4; matrix products, arithmetic and copies ran while one was open for 15% -> 14% of each run, Pallas kernels for 56% -> 61%
where the time goes in v1:
time: 255 us; the launch traced here: 254 us
  Pallas kernels  168 us (66%)
  other arithmetic  18.8 us (7%)
  local copies, waits for them, and re-layouts  18.6 us (7%)
  waiting for transfers between devices  17 us (7%)
  matrix products  10.5 us (4%)
  between operations  10.5 us (4%)
  starting transfers between devices  9.96 us (4%)
    pallas_call x3, Pallas kernels, tp_exchange(): pl.pallas_call(functools.partial(exchange_kernel, count, stride, tuple(mo...  74.6 us
    pallas_call x1, Pallas kernels, cache_attention(): pl.pallas_call(attention_kernel, out_shape=(jax.ShapeDtypeStruct((heads,...  64.1 us
    pallas_call x1, Pallas kernels, group_gather(): pl.pallas_call(functools.partial(gather_kernel, count), out_shape=tuple(s...  29.7 us
    ppermute x4, waiting for transfers between devices, branch(): return lambda t: jax.tree.map(lambda a: lax.ppermute(a, 'grp', pairs), t)  17 us
    unnamed x57, local copies, waits for them, and re-layouts  10.8 us
    pallas_call x2, other arithmetic, cache_attention(): pl.pallas_call(attention_kernel, out_shape=(jax.ShapeDtypeStruct((heads,...  5.54 us
    ppermute x3, starting transfers between devices, on_device(): w_received.append(lax.ppermute(send, 'tp', pairs))  5.22 us
  transfers between devices with their start and end apart: 7, of which 4 were waited for; matrix products, arithmetic and copies ran while one was open for 14% of the time, Pallas kernels for 61%

profile of v1, /device:TPU:4, one launch (start us, length us, event | category | flops | bytes accessed | tf_op | source)
XLA Modules:
  0.0 254.2 jit_solution(17508661912968494279)
XLA Ops:
  0.0 2.6 %constant_dynamic-slice_fusion.3 = (bf16[256,512]{1,0:T(8,128)(2,1)S(1)}, bf16[256,512]{1,0:T(8,128)(2,1)S(1)}, bf16[256,512]{1,0:T(8,128)(2,1)S(1)}, bf16[256,5...) fusion(bf16[256,4096]{1,0:T(8,128)(2,1)} %param.36, ...), kind=kLoop, calls=%fused_computation.64 | loop fusion | bytes 4194336 | tf_op jit(solution)/shard_map/dynamic_slice | solution.py:304
  3.5 1.6 collective-permute-start.20
  5.9 1.7 collective-permute-start.22
  8.5 2.0 collective-permute-start.21
  21.1 2.2 fusion
  26.2 4.4 %conditional.4 = (bf16[2,128,128]{2,1,0:T(8,128)(2,1)S(1)}) conditional(s32[]{:T(128)} %clamp.11, bf16[2,128,128]{2,1,0:T(8,128)(2,1)S(1)} %slice.133, bf16[2,128,128]{2,1,0:T(8,128)(2,1)S(1)} %slice.133, bf16[2,128,128]{2,1,0:T(8,128)(2,1)S(1)} %slice.133, bf16[2,128,128]{2,1,0:T(8,128)(2,1)S(1)} %slice.133, ...), branch_computations={%region_1.2_spmd, %region_2.3_spmd, %region_3.4_spmd, %region_4.5_... | conditional | bytes 393264 | solution.py:283
  26.3 1.3 collective-permute-start.1
  27.5 3.1 %collective-permute-done.1 = bf16[2,128,128]{2,1,0:T(8,128)(2,1)S(1)} collective-permute-done((bf16[2,128,128]{2,1,0:T(8,128)(2,1)S(1)}, bf16[2,128,128]{2,1,0:T(8,128)(2,1)S(1)}, u32[]{:S(2)}, u32[]{:S(2)}) %collective-permute-start.1) | collective-permute-done | bytes 65568 | tf_op jit(solution)/shard_map/cond/branch_2_fun/ppermute | solution.py:278
  30.6 5.5 %conditional.5 = (bf16[2,128,128]{2,1,0:T(8,128)(2,1)S(1)}) conditional(s32[]{:T(128)} %clamp.10, bf16[2,128,128]{2,1,0:T(8,128)(2,1)S(1)} %get-tuple-element.120, bf16[2,128,128]{2,1,0:T(8,128)(2,1)S(1)} %get-tuple-element.120, bf16[2,128,128]{2,1,0:T(8,128)(2,1)S(1)} %get-tuple-element.120, ...), branch_computations={%region_9.10_spmd, %region_10.11_spmd, %region_11.12_spmd, %region... | conditional | bytes 393264 | solution.py:285
  30.6 3.3 %collective-permute-start.8 = (bf16[2,128,128]{2,1,0:T(8,128)(2,1)S(1)}, bf16[2,128,128]{2,1,0:T(8,128)(2,1)S(1)}, u32[]{:S(2)}, u32[]{:S(2)}) collective-permute-start(bf16[2,128,128]{2,1,0:T(8,128)(2,1)S(1)} %param.10), channel_id=1, source_target_pairs={{0,128},{8,136},{16,144},{24,152},{32,160},{40,168},{48,176},{56,1... | collective-permute-start | bytes 196616 | tf_op jit(solution)/shard_map/cond/branch_2_fun/ppermute | solution.py:278
  33.9 2.2 collective-permute-done.8
  36.8 2.6 %convolution_convert_fusion = bf16[256,64]{0,1:T(8,128)(2,1)S(1)} fusion(bf16[4096,64]{0,1:T(8,128)(2,1)} %param.35, bf16[256,4096]{1,0:T(8,128)(2,1)} %param.32, f32[4096]{0:T(1024)S(1)} %copy-done.23, f32[256]{0:T(256)S(1)} %add_rsqrt_fusion), kind=kOutput, calls=%fused_computation.15 | convolution fusion | flops 138428416 | bytes 2671616 | tf_op jit(solution)/shard_map/dot_general | solution.py:323
  41.2 29.7 %shard_map.82 = (bf16[4,2,2,384,128]{4,3,2,1,0:T(8,128)(2,1)S(1)}, bf16[4,2,256,64]{3,2,1,0:T(8,128)(2,1)S(1)}) custom-call(bf16[2,384,128]{2,1,0:T(8,128)(2,1)S(1)} %copy-done.6, bf16[256,64]{1,0:T(8,128)(2,1)S(1)} %copy.80.refs_1_), custom_call_target="tpu_custom_call" | custom-call | tf_op jit(solution)/shard_map/pallas_call | solution.py:171
  73.7 1.4 copy-done.3
  75.1 64.1 %shard_map.83 = (f32[16,384,128]{2,1,0:T(8,128)S(1)}, f32[16,384,1]{2,1,0:T(8,128)}, f32[16,384,1]{2,1,0:T(8,128)}) custom-call(s32[3]{0:T(128)S(1)} %get-tuple-element.118.lo_ref, s32[3]{0:T(128)S(1)} %get-tuple-element.119.hi_ref, bf16[16,384,128]{2,1,0:T(8,128)(2,1)S(1)} %bitcast.67, bf16[1280,512]{1,0:T(8,128)(2,1)S(1)} %copy-done.5), custom_call_target="tpu_custom_call" | custom-call | tf_op jit(solution)/shard_map/pallas_call | solution.py:241
  139.2 1.5 convert_element_type.50
  140.7 2.8 %reduce = f32[16,384]{1,0:T(8,128)S(1)} reduce(f32[16,384,1]{2,1,0:T(8,128)} %get-tuple-element.67, f32[]{:T(128)} %constant.178), dimensions={2}, to_apply=%get-tuple-element.67.reduce_sub_computation | reduce | bytes 49156 | tf_op jit(solution)/shard_map/pallas_call | solution.py:241
  143.5 2.8 %reduce.1 = f32[16,384]{1,0:T(8,128)S(1)} reduce(f32[16,384,1]{2,1,0:T(8,128)} %get-tuple-element.68, f32[]{:T(128)} %constant.178), dimensions={2}, to_apply=%get-tuple-element.68.reduce_sub_computation | reduce | bytes 49156 | tf_op jit(solution)/shard_map/pallas_call | solution.py:241
  146.3 1.4 copy-done.1
  147.7 52.1 %shard_map.84 = (bf16[8,2,384,128]{3,2,1,0:T(8,128)(2,1)S(1)}, f32[8,2,384]{2,1,0:T(2,128)S(1)}, f32[8,2,384]{2,1,0:T(2,128)S(1)}) custom-call(bf16[8,2,384,128]{3,2,1,0:T(8,128)(2,1)S(1)} %bitcast.66, f32[8,2,384]{2,1,0:T(2,128)S(1)} %reshape.299.refs_1_, f32[8,2,384]{2,1,0:T(2,128)S(1)} %reshape.300.refs_2_), custom_call_target="tpu_custom_call" | custom-call | tf_op jit(solution)/shard_map/pallas_call | solution.py:89
  201.7 2.1 multiply_reduce_fusion
  204.6 5.4 %conditional.6 = (f32[2,130,128]{2,1,0:T(8,128)S(1)}) conditional(s32[]{:T(128)} %clamp.11, f32[2,130,128]{2,1,0:T(8,128)S(1)} %pad_maximum_fusion.4, f32[2,130,128]{2,1,0:T(8,128)S(1)} %pad_maximum_fusion.4, f32[2,130,128]{2,1,0:T(8,128)S(1)} %pad_maximum_fusion.4, ...), branch_computations={%region_16.17_spmd, %region_17.18_spmd, %region_18.19_spmd, %regio... | conditional | bytes 798768 | solution.py:283
  204.7 5.3 %collective-permute-done.11 = f32[2,130,128]{2,1,0:T(8,128)S(1)} collective-permute-done((f32[2,130,128]{2,1,0:T(8,128)S(1)}, f32[2,130,128]{2,1,0:T(8,128)S(1)}, u32[]{:S(2)}, u32[]{:S(2)}) %collective-permute-start.11) | collective-permute-done | bytes 133152 | tf_op jit(solution)/shard_map/cond/branch_2_fun/ppermute | solution.py:278
  210.1 6.8 %conditional.7 = (f32[2,130,128]{2,1,0:T(8,128)S(1)}) conditional(s32[]{:T(128)} %clamp.10, f32[2,130,128]{2,1,0:T(8,128)S(1)} %get-tuple-element.122, f32[2,130,128]{2,1,0:T(8,128)S(1)} %get-tuple-element.122, f32[2,130,128]{2,1,0:T(8,128)S(1)} %get-tuple-element.122, f32[2,130,128]{2,1,0:T(8,128)S(1)} %get-tuple-element.122), branch_computations={%region_24.25_spmd, %region_25.26_spmd, %region_26.27_spmd, %regio... | conditional | bytes 798768 | solution.py:285
  210.2 6.4 %collective-permute-done.18 = f32[2,130,128]{2,1,0:T(8,128)S(1)} collective-permute-done((f32[2,130,128]{2,1,0:T(8,128)S(1)}, f32[2,130,128]{2,1,0:T(8,128)S(1)}, u32[]{:S(2)}, u32[]{:S(2)}) %collective-permute-start.18) | collective-permute-done | bytes 133152 | tf_op jit(solution)/shard_map/cond/branch_2_fun/ppermute | solution.py:278
  219.8 1.6 copy.99
  223.0 1.2 fusion.60
  226.4 9.0 %shard_map.85 = bf16[4,256,256]{2,1,0:T(8,128)(2,1)S(1)} custom-call(bf16[256,256]{1,0:T(8,128)(2,1)S(1)} %copy.93.refs_0_), custom_call_target="tpu_custom_call" | custom-call | tf_op jit(solution)/shard_map/pallas_call | solution.py:89
  235.8 1.3 fusion.20
  237.1 1.3 convolution_add_fusion.1
  238.5 1.4 fusion.3
  239.9 13.5 %shard_map.86 = bf16[2,256,512]{2,1,0:T(8,128)(2,1)S(1)} custom-call(bf16[256,512]{1,0:T(8,128)(2,1)S(1)} %slice.161.refs_0_), custom_call_target="tpu_custom_call" | custom-call | tf_op jit(solution)/shard_map/pallas_call | solution.py:89
  (107 shorter events, 21.8 us)
Async XLA Ops:
  0.0 23.4 %copy-start = (bf16[4096,256]{1,0:T(8,128)(2,1)S(1)}, bf16[4096,256]{1,0:T(8,128)(2,1)}, u32[]{:S(2)}) copy-start(bf16[4096,256]{1,0:T(8,128)(2,1)} %param.34) | copy-start | bytes 6291460
  2.6 7.9 %copy-start.22 = (s32[32]{0:T(128)S(1)}, s32[32]{0:T(128)}, u32[]{:S(2)}) copy-start(s32[32]{0:T(128)} %param.39) | copy-start | bytes 388
  2.6 11.7 %copy-start.24 = (s32[64]{0:T(128)S(1)}, s32[64]{0:T(128)}, u32[]{:S(2)}) copy-start(s32[64]{0:T(128)} %param.38) | copy-start | bytes 772
  3.5 233.6 %collective-permute-start.20 = (bf16[256,1024]{1,0:T(8,128)(2,1)}, bf16[256,1024]{1,0:T(8,128)(2,1)}, u32[]{:S(2)}, u32[]{:S(2)}) collective-permute-start(bf16[256,1024]{1,0:T(8,128)(2,1)} %pad_maximum_fusion), channel_id=1, source_target_pairs={{0,2},{1,3},{2,4},{3,5},{4,6},{5,7},{6,0},{7,1},{8,10},{9,11},{10,... | collective-permute-start | bytes 1572872 | tf_op jit(solution)/shard_map/ppermute | solution.py:312
  5.1 18.3 %copy-start.23 = (f32[4096]{0:T(1024)S(1)}, f32[4096]{0:T(1024)}, u32[]{:S(2)}) copy-start(f32[4096]{0:T(1024)} %param.33) | copy-start | bytes 49156
  5.9 229.8 %collective-permute-start.22 = (bf16[256,1024]{1,0:T(8,128)(2,1)}, bf16[256,1024]{1,0:T(8,128)(2,1)}, u32[]{:S(2)}, u32[]{:S(2)}) collective-permute-start(bf16[256,1024]{1,0:T(8,128)(2,1)} %pad_maximum_fusion.2), channel_id=1, source_target_pairs={{0,6},{1,7},{2,0},{3,1},{4,2},{5,3},{6,4},{7,5},{8,14},{9,15},{10,... | collective-permute-start | bytes 1572872 | tf_op jit(solution)/shard_map/ppermute | solution.py:312
  8.5 230.0 %collective-permute-start.21 = (bf16[256,1024]{1,0:T(8,128)(2,1)}, bf16[256,1024]{1,0:T(8,128)(2,1)}, u32[]{:S(2)}, u32[]{:S(2)}) collective-permute-start(bf16[256,1024]{1,0:T(8,128)(2,1)} %pad_maximum_fusion.1), channel_id=1, source_target_pairs={{0,4},{1,5},{2,6},{3,7},{4,0},{5,1},{6,2},{7,3},{8,12},{9,13},{10,... | collective-permute-start | bytes 1572872 | tf_op jit(solution)/shard_map/ppermute | solution.py:312
  21.1 2.3 copy-start.9
  25.4 0.7 copy-start.12
  25.4 0.7 copy-start.14
  26.2 9.9 %copy-start.10 = (bf16[2,256,128]{2,1,0:T(8,128)(2,1)}, bf16[2,256,128]{2,1,0:T(8,128)(2,1)S(1)}, u32[]{:S(2)}) copy-start(bf16[2,256,128]{2,1,0:T(8,128)(2,1)S(1)} %maximum_bitcast_fusion) | copy-start | bytes 393220
  26.3 4.4 %collective-permute-start.1 = (bf16[2,128,128]{2,1,0:T(8,128)(2,1)S(1)}, bf16[2,128,128]{2,1,0:T(8,128)(2,1)S(1)}, u32[]{:S(2)}, u32[]{:S(2)}) collective-permute-start(bf16[2,128,128]{2,1,0:T(8,128)(2,1)S(1)} %param.2), channel_id=1, source_target_pairs={{0,16},{8,24},{16,0},{24,8},{32,48},{40,56},{48,32},{56,40},{64,80... | collective-permute-start | bytes 196616 | tf_op jit(solution)/shard_map/cond/branch_2_fun/ppermute | solution.py:278
  30.6 5.5 %collective-permute-start.8 = (bf16[2,128,128]{2,1,0:T(8,128)(2,1)S(1)}, bf16[2,128,128]{2,1,0:T(8,128)(2,1)S(1)}, u32[]{:S(2)}, u32[]{:S(2)}) collective-permute-start(bf16[2,128,128]{2,1,0:T(8,128)(2,1)S(1)} %param.10), channel_id=1, source_target_pairs={{0,128},{8,136},{16,144},{24,152},{32,160},{40,168},{48,176},{56,1... | collective-permute-start | bytes 196616 | tf_op jit(solution)/shard_map/cond/branch_2_fun/ppermute | solution.py:278
  36.8 36.9 %copy-start.5 = (bf16[1280,512]{1,0:T(8,128)(2,1)S(1)}, bf16[1280,512]{1,0:T(8,128)(2,1)}, u32[]{:S(2)}) copy-start(bf16[1280,512]{1,0:T(8,128)(2,1)} %cache_ref.1) | copy-start | bytes 3932164
  40.3 0.9 copy-start.6
  70.9 1.2 copy-start.2
  72.1 0.8 copy-start.7
  73.7 1.4 copy-start.3
  146.3 1.4 copy-start.1
  199.9 1.2 copy-start.4
  203.8 13.6 %copy-start.8 = (bf16[4,2,256,64]{3,2,1,0:T(8,128)(2,1)S(1)}, bf16[4,2,256,64]{3,2,1,0:T(8,128)(2,1)}, u32[]{:S(2)}) copy-start(bf16[4,2,256,64]{3,2,1,0:T(8,128)(2,1)} %copy-done.7) | copy-start | bytes 786436
  204.6 5.4 %collective-permute-start.11 = (f32[2,130,128]{2,1,0:T(8,128)S(1)}, f32[2,130,128]{2,1,0:T(8,128)S(1)}, u32[]{:S(2)}, u32[]{:S(2)}) collective-permute-start(f32[2,130,128]{2,1,0:T(8,128)S(1)} %param.14), channel_id=1, source_target_pairs={{0,16},{8,24},{16,0},{24,8},{32,48},{40,56},{48,32},{56,40},{64,80... | collective-permute-start | bytes 399368 | tf_op jit(solution)/shard_map/cond/branch_2_fun/ppermute | solution.py:278
  210.0 12.0 %copy-start.13 = (f32[256,64]{1,0:T(8,128)S(1)}, f32[256,64]{1,0:T(8,128)}, u32[]{:S(2)}) copy-start(f32[256,64]{1,0:T(8,128)} %copy-done.12) | copy-start | bytes 196612
  210.0 12.0 %copy-start.15 = (f32[256,64]{1,0:T(8,128)S(1)}, f32[256,64]{1,0:T(8,128)}, u32[]{:S(2)}) copy-start(f32[256,64]{1,0:T(8,128)} %copy-done.14) | copy-start | bytes 196612
  210.1 6.5 %collective-permute-start.18 = (f32[2,130,128]{2,1,0:T(8,128)S(1)}, f32[2,130,128]{2,1,0:T(8,128)S(1)}, u32[]{:S(2)}, u32[]{:S(2)}) collective-permute-start(f32[2,130,128]{2,1,0:T(8,128)S(1)} %param.22), channel_id=1, source_target_pairs={{0,128},{8,136},{16,144},{24,152},{32,160},{40,168},{48,176},{56,1... | collective-permute-start | bytes 399368 | tf_op jit(solution)/shard_map/cond/branch_2_fun/ppermute | solution.py:278
  217.5 5.5 %copy-start.11 = (bf16[2,256,128]{2,1,0:T(8,128)(2,1)S(1)}, bf16[2,256,128]{2,1,0:T(8,128)(2,1)}, u32[]{:S(2)}) copy-start(bf16[2,256,128]{2,1,0:T(8,128)(2,1)} %copy-done.10) | copy-start | bytes 393220
  218.4 3.0 %copy-start.20 = (f32[2,1,128]{2,1,0:T(1,128)S(1)}, f32[2,1,128]{2,1,0:T(1,128)}, u32[]{:S(2)}) copy-start(f32[2,1,128]{2,1,0:T(1,128)} %get-tuple-element.101) | copy-start | bytes 3076
  218.4 3.0 %copy-start.21 = (f32[2,1,128]{2,1,0:T(1,128)S(1)}, f32[2,1,128]{2,1,0:T(1,128)}, u32[]{:S(2)}) copy-start(f32[2,1,128]{2,1,0:T(1,128)} %get-tuple-element.102) | copy-start | bytes 3076
  222.0 2.3 copy-start.18
  222.0 2.3 copy-start.19
  223.0 12.5 %copy-start.16 = (bf16[256,512]{1,0:T(8,128)(2,1)S(1)}, bf16[256,512]{1,0:T(8,128)(2,1)}, u32[]{:S(2)}) copy-start(bf16[256,512]{1,0:T(8,128)(2,1)} %get-tuple-element.86) | copy-start | bytes 786436
  223.0 12.5 %copy-start.17 = (bf16[256,512]{1,0:T(8,128)(2,1)S(1)}, bf16[256,512]{1,0:T(8,128)(2,1)}, u32[]{:S(2)}) copy-start(bf16[256,512]{1,0:T(8,128)(2,1)} %get-tuple-element.87) | copy-start | bytes 786436

commit v2 on v1

--- a/solution.py
+++ b/solution.py
@@ -16,7 +16,7 @@
 THETA = 5000000.0
 EPS = 1e-05
 NEG = -1e30
-CHUNK = 128
+CHUNK = 640
 MESH = pl.DeviceIdType.MESH
 
 

time: 255 us -> 212 us (0.83)
  Pallas kernels: 168 us -> 121 us
    pallas_call x1, Pallas kernels: 64.1 us -> 20.5 us  [cache_attention(): pl.pallas_call(attention_kernel, out_shape=(jax.ShapeDtypeStruct((heads,...]
    pallas_call x3, Pallas kernels: 74.6 us -> 71.2 us  [tp_exchange(): pl.pallas_call(functools.partial(exchange_kernel, count, stride, tuple(mo...]
  transfers between devices with their start and end apart: 7 -> 7, of which waited for: 4 -> 4; matrix products, arithmetic and copies ran while one was open for 14% -> 17% of each run, Pallas kernels for 61% -> 51%
where the time goes in v2:
time: 212 us; the launch traced here: 209 us
  Pallas kernels  121 us (57%)
  waiting for transfers between devices  19.4 us (9%)
  other arithmetic  18.8 us (9%)
  local copies, waits for them, and re-layouts  18.6 us (9%)
  matrix products  10.5 us (5%)
  between operations  10.5 us (5%)
  starting transfers between devices  9.93 us (5%)
    pallas_call x3, Pallas kernels, tp_exchange(): pl.pallas_call(functools.partial(exchange_kernel, count, stride, tuple(mo...  71.2 us
    pallas_call x1, Pallas kernels, group_gather(): pl.pallas_call(functools.partial(gather_kernel, count), out_shape=tuple(s...  29.7 us
    pallas_call x1, Pallas kernels, cache_attention(): pl.pallas_call(attention_kernel, out_shape=(jax.ShapeDtypeStruct((heads,...  20.5 us
    ppermute x4, waiting for transfers between devices, branch(): return lambda t: jax.tree.map(lambda a: lax.ppermute(a, 'grp', pairs), t)  19.3 us
    unnamed x57, local copies, waits for them, and re-layouts  10.8 us
    pallas_call x2, other arithmetic, cache_attention(): pl.pallas_call(attention_kernel, out_shape=(jax.ShapeDtypeStruct((heads,...  5.54 us
    ppermute x3, starting transfers between devices, on_device(): w_received.append(lax.ppermute(send, 'tp', pairs))  5.22 us
    ppermute x4, starting transfers between devices, branch(): return lambda t: jax.tree.map(lambda a: lax.ppermute(a, 'grp', pairs), t)  4.71 us
  transfers between devices with their start and end apart: 7, of which 4 were waited for; matrix products, arithmetic and copies ran while one was open for 17% of the time, Pallas kernels for 51%

profile of v2, /device:TPU:4, one launch (start us, length us, event | category | flops | bytes accessed | tf_op | source)
XLA Modules:
  0.0 209.4 jit_solution(8887012121309395058)
XLA Ops:
  0.0 2.6 %constant_dynamic-slice_fusion.3 = (bf16[256,512]{1,0:T(8,128)(2,1)S(1)}, bf16[256,512]{1,0:T(8,128)(2,1)S(1)}, bf16[256,512]{1,0:T(8,128)(2,1)S(1)}, bf16[256,5...) fusion(bf16[256,4096]{1,0:T(8,128)(2,1)} %param.36, ...), kind=kLoop, calls=%fused_computation.64 | loop fusion | bytes 4194336 | tf_op jit(solution)/shard_map/dynamic_slice | solution.py:304
  3.5 1.6 collective-permute-start.20
  5.9 1.7 collective-permute-start.22
  8.5 2.0 collective-permute-start.21
  21.1 2.2 %fusion = f32[256]{0:T(256)S(1)} fusion(bf16[256,4096]{1,0:T(8,128)(2,1)} %param.32), kind=kLoop, calls=%fused_computation.2 | loop fusion | flops 3145472 | bytes 2098176 | tf_op jit(solution)/shard_map/reduce_sum | solution.py:317
  26.2 5.9 %conditional.4 = (bf16[2,128,128]{2,1,0:T(8,128)(2,1)S(1)}) conditional(s32[]{:T(128)} %clamp.11, bf16[2,128,128]{2,1,0:T(8,128)(2,1)S(1)} %slice.133, bf16[2,128,128]{2,1,0:T(8,128)(2,1)S(1)} %slice.133, bf16[2,128,128]{2,1,0:T(8,128)(2,1)S(1)} %slice.133, bf16[2,128,128]{2,1,0:T(8,128)(2,1)S(1)} %slice.133, ...), branch_computations={%region_1.2_spmd, %region_2.3_spmd, %region_3.4_spmd, %region_4.5_... | conditional | bytes 393264 | solution.py:283
  26.9 5.3 %collective-permute-done.3 = bf16[2,128,128]{2,1,0:T(8,128)(2,1)S(1)} collective-permute-done((bf16[2,128,128]{2,1,0:T(8,128)(2,1)S(1)}, bf16[2,128,128]{2,1,0:T(8,128)(2,1)S(1)}, u32[]{:S(2)}, u32[]{:S(2)}) %collective-permute-start.3) | collective-permute-done | bytes 65568 | tf_op jit(solution)/shard_map/cond/branch_4_fun/ppermute | solution.py:278
  32.1 5.5 %conditional.5 = (bf16[2,128,128]{2,1,0:T(8,128)(2,1)S(1)}) conditional(s32[]{:T(128)} %clamp.10, bf16[2,128,128]{2,1,0:T(8,128)(2,1)S(1)} %get-tuple-element.120, bf16[2,128,128]{2,1,0:T(8,128)(2,1)S(1)} %get-tuple-element.120, bf16[2,128,128]{2,1,0:T(8,128)(2,1)S(1)} %get-tuple-element.120, ...), branch_computations={%region_9.10_spmd, %region_10.11_spmd, %region_11.12_spmd, %region... | conditional | bytes 393264 | solution.py:285
  32.1 3.3 %collective-permute-start.8 = (bf16[2,128,128]{2,1,0:T(8,128)(2,1)S(1)}, bf16[2,128,128]{2,1,0:T(8,128)(2,1)S(1)}, u32[]{:S(2)}, u32[]{:S(2)}) collective-permute-start(bf16[2,128,128]{2,1,0:T(8,128)(2,1)S(1)} %param.10), channel_id=1, source_target_pairs={{0,128},{8,136},{16,144},{24,152},{32,160},{40,168},{48,176},{56,1... | collective-permute-start | bytes 196616 | tf_op jit(solution)/shard_map/cond/branch_2_fun/ppermute | solution.py:278
  35.4 2.2 %collective-permute-done.8 = bf16[2,128,128]{2,1,0:T(8,128)(2,1)S(1)} collective-permute-done((bf16[2,128,128]{2,1,0:T(8,128)(2,1)S(1)}, bf16[2,128,128]{2,1,0:T(8,128)(2,1)S(1)}, u32[]{:S(2)}, u32[]{:S(2)}) %collective-permute-start.8) | collective-permute-done | bytes 65568 | tf_op jit(solution)/shard_map/cond/branch_2_fun/ppermute | solution.py:278
  38.3 2.6 %convolution_convert_fusion = bf16[256,64]{0,1:T(8,128)(2,1)S(1)} fusion(bf16[4096,64]{0,1:T(8,128)(2,1)} %param.35, bf16[256,4096]{1,0:T(8,128)(2,1)} %param.32, f32[4096]{0:T(1024)S(1)} %copy-done.23, f32[256]{0:T(256)S(1)} %add_rsqrt_fusion), kind=kOutput, calls=%fused_computation.15 | convolution fusion | flops 138428416 | bytes 2671616 | tf_op jit(solution)/shard_map/dot_general | solution.py:323
  42.7 29.7 %shard_map.82 = (bf16[4,2,2,384,128]{4,3,2,1,0:T(8,128)(2,1)S(1)}, bf16[4,2,256,64]{3,2,1,0:T(8,128)(2,1)S(1)}) custom-call(bf16[2,384,128]{2,1,0:T(8,128)(2,1)S(1)} %copy-done.6, bf16[256,64]{1,0:T(8,128)(2,1)S(1)} %copy.80.refs_1_), custom_call_target="tpu_custom_call" | custom-call | tf_op jit(solution)/shard_map/pallas_call | solution.py:171
  75.2 1.4 copy-done.3
  76.6 20.5 %shard_map.83 = (f32[16,384,128]{2,1,0:T(8,128)S(1)}, f32[16,384,1]{2,1,0:T(8,128)}, f32[16,384,1]{2,1,0:T(8,128)}) custom-call(s32[3]{0:T(128)S(1)} %get-tuple-element.118.lo_ref, s32[3]{0:T(128)S(1)} %get-tuple-element.119.hi_ref, bf16[16,384,128]{2,1,0:T(8,128)(2,1)S(1)} %bitcast.67, bf16[1280,512]{1,0:T(8,128)(2,1)S(1)} %copy-done.5), custom_call_target="tpu_custom_call" | custom-call | tf_op jit(solution)/shard_map/pallas_call | solution.py:241
  97.1 1.5 convert_element_type.50
  98.5 2.8 %reduce = f32[16,384]{1,0:T(8,128)S(1)} reduce(f32[16,384,1]{2,1,0:T(8,128)} %get-tuple-element.67, f32[]{:T(128)} %constant.178), dimensions={2}, to_apply=%get-tuple-element.67.reduce_sub_computation | reduce | bytes 49156 | tf_op jit(solution)/shard_map/pallas_call | solution.py:241
  101.3 2.8 %reduce.1 = f32[16,384]{1,0:T(8,128)S(1)} reduce(f32[16,384,1]{2,1,0:T(8,128)} %get-tuple-element.68, f32[]{:T(128)} %constant.178), dimensions={2}, to_apply=%get-tuple-element.68.reduce_sub_computation | reduce | bytes 49156 | tf_op jit(solution)/shard_map/pallas_call | solution.py:241
  104.2 1.4 copy-done.1
  105.6 48.3 %shard_map.84 = (bf16[8,2,384,128]{3,2,1,0:T(8,128)(2,1)S(1)}, f32[8,2,384]{2,1,0:T(2,128)S(1)}, f32[8,2,384]{2,1,0:T(2,128)S(1)}) custom-call(bf16[8,2,384,128]{3,2,1,0:T(8,128)(2,1)S(1)} %bitcast.66, f32[8,2,384]{2,1,0:T(2,128)S(1)} %reshape.299.refs_1_, f32[8,2,384]{2,1,0:T(2,128)S(1)} %reshape.300.refs_2_), custom_call_target="tpu_custom_call" | custom-call | tf_op jit(solution)/shard_map/pallas_call | solution.py:89
  155.7 2.1 %multiply_reduce_fusion = f32[2,384,128]{2,1,0:T(8,128)S(1)} fusion(bf16[8,2,384,128]{3,2,1,0:T(8,128)(2,1)} %copy-done.4, f32[8,2,384]{2,1,0:T(2,128)S(1)} %get-tuple-element.81), kind=kLoop, calls=%fused_computation.5 | loop fusion | flops 2260992 | bytes 1990656 | tf_op jit(solution)/shard_map/reduce_sum | solution.py:357
  158.6 6.7 %conditional.6 = (f32[2,130,128]{2,1,0:T(8,128)S(1)}) conditional(s32[]{:T(128)} %clamp.11, f32[2,130,128]{2,1,0:T(8,128)S(1)} %pad_maximum_fusion.4, f32[2,130,128]{2,1,0:T(8,128)S(1)} %pad_maximum_fusion.4, f32[2,130,128]{2,1,0:T(8,128)S(1)} %pad_maximum_fusion.4, ...), branch_computations={%region_16.17_spmd, %region_17.18_spmd, %region_18.19_spmd, %regio... | conditional | bytes 798768 | solution.py:283
  158.7 6.5 %collective-permute-done.13 = f32[2,130,128]{2,1,0:T(8,128)S(1)} collective-permute-done((f32[2,130,128]{2,1,0:T(8,128)S(1)}, f32[2,130,128]{2,1,0:T(8,128)S(1)}, u32[]{:S(2)}, u32[]{:S(2)}) %collective-permute-start.13) | collective-permute-done | bytes 133152 | tf_op jit(solution)/shard_map/cond/branch_4_fun/ppermute | solution.py:278
  165.3 6.3 %conditional.7 = (f32[2,130,128]{2,1,0:T(8,128)S(1)}) conditional(s32[]{:T(128)} %clamp.10, f32[2,130,128]{2,1,0:T(8,128)S(1)} %get-tuple-element.122, f32[2,130,128]{2,1,0:T(8,128)S(1)} %get-tuple-element.122, f32[2,130,128]{2,1,0:T(8,128)S(1)} %get-tuple-element.122, f32[2,130,128]{2,1,0:T(8,128)S(1)} %get-tuple-element.122), branch_computations={%region_24.25_spmd, %region_25.26_spmd, %region_26.27_spmd, %regio... | conditional | bytes 798768 | solution.py:285
  166.1 5.3 %collective-permute-done.18 = f32[2,130,128]{2,1,0:T(8,128)S(1)} collective-permute-done((f32[2,130,128]{2,1,0:T(8,128)S(1)}, f32[2,130,128]{2,1,0:T(8,128)S(1)}, u32[]{:S(2)}, u32[]{:S(2)}) %collective-permute-start.18) | collective-permute-done | bytes 133152 | tf_op jit(solution)/shard_map/cond/branch_2_fun/ppermute | solution.py:278
  174.6 1.6 copy.99
  177.8 1.2 fusion.60
  179.8 1.2 fusion.7
  181.1 8.1 %shard_map.85 = bf16[4,256,256]{2,1,0:T(8,128)(2,1)S(1)} custom-call(bf16[256,256]{1,0:T(8,128)(2,1)S(1)} %copy.93.refs_0_), custom_call_target="tpu_custom_call" | custom-call | tf_op jit(solution)/shard_map/pallas_call | solution.py:89
  189.6 1.3 fusion.20
  191.0 1.4 convolution_add_fusion.1
  192.4 1.4 fusion.3
  193.8 14.8 %shard_map.86 = bf16[2,256,512]{2,1,0:T(8,128)(2,1)S(1)} custom-call(bf16[256,512]{1,0:T(8,128)(2,1)S(1)} %slice.161.refs_0_), custom_call_target="tpu_custom_call" | custom-call | tf_op jit(solution)/shard_map/pallas_call | solution.py:89
  (107 shorter events, 21.8 us)
Async XLA Ops:
  0.0 23.4 %copy-start = (bf16[4096,256]{1,0:T(8,128)(2,1)S(1)}, bf16[4096,256]{1,0:T(8,128)(2,1)}, u32[]{:S(2)}) copy-start(bf16[4096,256]{1,0:T(8,128)(2,1)} %param.34) | copy-start | bytes 6291460
  2.6 7.9 %copy-start.22 = (s32[32]{0:T(128)S(1)}, s32[32]{0:T(128)}, u32[]{:S(2)}) copy-start(s32[32]{0:T(128)} %param.39) | copy-start | bytes 388
  2.6 11.7 %copy-start.24 = (s32[64]{0:T(128)S(1)}, s32[64]{0:T(128)}, u32[]{:S(2)}) copy-start(s32[64]{0:T(128)} %param.38) | copy-start | bytes 772
  3.5 187.5 %collective-permute-start.20 = (bf16[256,1024]{1,0:T(8,128)(2,1)}, bf16[256,1024]{1,0:T(8,128)(2,1)}, u32[]{:S(2)}, u32[]{:S(2)}) collective-permute-start(bf16[256,1024]{1,0:T(8,128)(2,1)} %pad_maximum_fusion), channel_id=1, source_target_pairs={{0,2},{1,3},{2,4},{3,5},{4,6},{5,7},{6,0},{7,1},{8,10},{9,11},{10,... | collective-permute-start | bytes 1572872 | tf_op jit(solution)/shard_map/ppermute | solution.py:312
  5.1 18.3 %copy-start.23 = (f32[4096]{0:T(1024)S(1)}, f32[4096]{0:T(1024)}, u32[]{:S(2)}) copy-start(f32[4096]{0:T(1024)} %param.33) | copy-start | bytes 49156
  5.9 183.7 %collective-permute-start.22 = (bf16[256,1024]{1,0:T(8,128)(2,1)}, bf16[256,1024]{1,0:T(8,128)(2,1)}, u32[]{:S(2)}, u32[]{:S(2)}) collective-permute-start(bf16[256,1024]{1,0:T(8,128)(2,1)} %pad_maximum_fusion.2), channel_id=1, source_target_pairs={{0,6},{1,7},{2,0},{3,1},{4,2},{5,3},{6,4},{7,5},{8,14},{9,15},{10,... | collective-permute-start | bytes 1572872 | tf_op jit(solution)/shard_map/ppermute | solution.py:312
  8.5 183.9 %collective-permute-start.21 = (bf16[256,1024]{1,0:T(8,128)(2,1)}, bf16[256,1024]{1,0:T(8,128)(2,1)}, u32[]{:S(2)}, u32[]{:S(2)}) collective-permute-start(bf16[256,1024]{1,0:T(8,128)(2,1)} %pad_maximum_fusion.1), channel_id=1, source_target_pairs={{0,4},{1,5},{2,6},{3,7},{4,0},{5,1},{6,2},{7,3},{8,12},{9,13},{10,... | collective-permute-start | bytes 1572872 | tf_op jit(solution)/shard_map/ppermute | solution.py:312
  21.1 2.3 %copy-start.9 = (bf16[256,4096]{1,0:T(8,128)(2,1)S(1)}, bf16[256,4096]{1,0:T(8,128)(2,1)}, u32[]{:S(2)}) copy-start(bf16[256,4096]{1,0:T(8,128)(2,1)} %param.32) | copy-start | bytes 6291460
  25.4 0.7 copy-start.12
  25.4 0.7 copy-start.14
  26.2 11.4 %copy-start.10 = (bf16[2,256,128]{2,1,0:T(8,128)(2,1)}, bf16[2,256,128]{2,1,0:T(8,128)(2,1)S(1)}, u32[]{:S(2)}) copy-start(bf16[2,256,128]{2,1,0:T(8,128)(2,1)S(1)} %maximum_bitcast_fusion) | copy-start | bytes 393220
  26.3 5.9 %collective-permute-start.3 = (bf16[2,128,128]{2,1,0:T(8,128)(2,1)S(1)}, bf16[2,128,128]{2,1,0:T(8,128)(2,1)S(1)}, u32[]{:S(2)}, u32[]{:S(2)}) collective-permute-start(bf16[2,128,128]{2,1,0:T(8,128)(2,1)S(1)} %param.4), channel_id=1, source_target_pairs={{0,32},{8,40},{16,48},{24,56},{32,0},{40,8},{48,16},{56,24},{64,96... | collective-permute-start | bytes 196616 | tf_op jit(solution)/shard_map/cond/branch_4_fun/ppermute | solution.py:278
  32.1 5.5 %collective-permute-start.8 = (bf16[2,128,128]{2,1,0:T(8,128)(2,1)S(1)}, bf16[2,128,128]{2,1,0:T(8,128)(2,1)S(1)}, u32[]{:S(2)}, u32[]{:S(2)}) collective-permute-start(bf16[2,128,128]{2,1,0:T(8,128)(2,1)S(1)} %param.10), channel_id=1, source_target_pairs={{0,128},{8,136},{16,144},{24,152},{32,160},{40,168},{48,176},{56,1... | collective-permute-start | bytes 196616 | tf_op jit(solution)/shard_map/cond/branch_2_fun/ppermute | solution.py:278
  38.3 36.8 %copy-start.5 = (bf16[1280,512]{1,0:T(8,128)(2,1)S(1)}, bf16[1280,512]{1,0:T(8,128)(2,1)}, u32[]{:S(2)}) copy-start(bf16[1280,512]{1,0:T(8,128)(2,1)} %cache_ref.1) | copy-start | bytes 3932164
  41.8 0.9 copy-start.6
  72.4 1.2 copy-start.2
  73.6 0.8 copy-start.7
  75.2 1.4 copy-start.3
  104.2 1.4 copy-start.1
  153.9 1.2 copy-start.4
  157.8 14.4 %copy-start.8 = (bf16[4,2,256,64]{3,2,1,0:T(8,128)(2,1)S(1)}, bf16[4,2,256,64]{3,2,1,0:T(8,128)(2,1)}, u32[]{:S(2)}) copy-start(bf16[4,2,256,64]{3,2,1,0:T(8,128)(2,1)} %copy-done.7) | copy-start | bytes 786436
  158.6 6.6 %collective-permute-start.13 = (f32[2,130,128]{2,1,0:T(8,128)S(1)}, f32[2,130,128]{2,1,0:T(8,128)S(1)}, u32[]{:S(2)}, u32[]{:S(2)}) collective-permute-start(f32[2,130,128]{2,1,0:T(8,128)S(1)} %param.16), channel_id=1, source_target_pairs={{0,32},{8,40},{16,48},{24,56},{32,0},{40,8},{48,16},{56,24},{64,96... | collective-permute-start | bytes 399368 | tf_op jit(solution)/shard_map/cond/branch_4_fun/ppermute | solution.py:278
  165.3 11.5 %copy-start.13 = (f32[256,64]{1,0:T(8,128)S(1)}, f32[256,64]{1,0:T(8,128)}, u32[]{:S(2)}) copy-start(f32[256,64]{1,0:T(8,128)} %copy-done.12) | copy-start | bytes 196612
  165.3 11.5 %copy-start.15 = (f32[256,64]{1,0:T(8,128)S(1)}, f32[256,64]{1,0:T(8,128)}, u32[]{:S(2)}) copy-start(f32[256,64]{1,0:T(8,128)} %copy-done.14) | copy-start | bytes 196612
  165.3 6.0 %collective-permute-start.18 = (f32[2,130,128]{2,1,0:T(8,128)S(1)}, f32[2,130,128]{2,1,0:T(8,128)S(1)}, u32[]{:S(2)}, u32[]{:S(2)}) collective-permute-start(f32[2,130,128]{2,1,0:T(8,128)S(1)} %param.22), channel_id=1, source_target_pairs={{0,128},{8,136},{16,144},{24,152},{32,160},{40,168},{48,176},{56,1... | collective-permute-start | bytes 399368 | tf_op jit(solution)/shard_map/cond/branch_2_fun/ppermute | solution.py:278
  172.3 5.5 %copy-start.11 = (bf16[2,256,128]{2,1,0:T(8,128)(2,1)S(1)}, bf16[2,256,128]{2,1,0:T(8,128)(2,1)}, u32[]{:S(2)}) copy-start(bf16[2,256,128]{2,1,0:T(8,128)(2,1)} %copy-done.10) | copy-start | bytes 393220
  173.2 3.0 %copy-start.20 = (f32[2,1,128]{2,1,0:T(1,128)S(1)}, f32[2,1,128]{2,1,0:T(1,128)}, u32[]{:S(2)}) copy-start(f32[2,1,128]{2,1,0:T(1,128)} %get-tuple-element.101) | copy-start | bytes 3076
  173.2 3.0 %copy-start.21 = (f32[2,1,128]{2,1,0:T(1,128)S(1)}, f32[2,1,128]{2,1,0:T(1,128)}, u32[]{:S(2)}) copy-start(f32[2,1,128]{2,1,0:T(1,128)} %get-tuple-element.102) | copy-start | bytes 3076
  176.8 2.3 %copy-start.18 = (f32[2,128]{1,0:T(2,128)S(1)}, f32[2,128]{1,0:T(2,128)}, u32[]{:S(2)}) copy-start(f32[2,128]{1,0:T(2,128)} %get-tuple-element.77) | copy-start | bytes 3076
  176.8 2.3 %copy-start.19 = (f32[2,128]{1,0:T(2,128)S(1)}, f32[2,128]{1,0:T(2,128)}, u32[]{:S(2)}) copy-start(f32[2,128]{1,0:T(2,128)} %get-tuple-element.78) | copy-start | bytes 3076
  177.7 11.6 %copy-start.16 = (bf16[256,512]{1,0:T(8,128)(2,1)S(1)}, bf16[256,512]{1,0:T(8,128)(2,1)}, u32[]{:S(2)}) copy-start(bf16[256,512]{1,0:T(8,128)(2,1)} %get-tuple-element.86) | copy-start | bytes 786436
  177.8 11.6 %copy-start.17 = (bf16[256,512]{1,0:T(8,128)(2,1)S(1)}, bf16[256,512]{1,0:T(8,128)(2,1)}, u32[]{:S(2)}) copy-start(bf16[256,512]{1,0:T(8,128)(2,1)} %get-tuple-element.87) | copy-start | bytes 786436

commit v3 on v2

--- a/solution.py
+++ b/solution.py
@@ -187,7 +187,7 @@
     )(*arrays)
 
 
-def attention_kernel(lo_ref, hi_ref, q_ref, cache_ref, mix_ref, peak_ref, total_ref):
+def attention_kernel(lo_ref, hi_ref, q_ref, cache_ref, mix_ref, peak_ref, total_ref, keys_t):
     block = pl.program_id(0)
     kv_head = pl.program_id(1)
     lo = lo_ref[block]
@@ -197,6 +197,7 @@
     value_col = pl.multiple_of((KVH + kv_head) * HD, HD)
     first = lo // CHUNK
     last = jnp.where(hi > lo, (hi + CHUNK - 1) // CHUNK, first)
+    keys_t[...] = cache_ref[:, pl.ds(key_col, HD)].astype(jnp.float32).T.astype(jnp.bfloat16)
 
     def one_head(head, carry):
         query = q_ref[head]
@@ -204,12 +205,11 @@
         def body(chunk, state):
             peak, total, mix = state
             start = pl.multiple_of(chunk * CHUNK, CHUNK)
-            keys = cache_ref[pl.ds(start, CHUNK), pl.ds(key_col, HD)]
             values = cache_ref[pl.ds(start, CHUNK), pl.ds(value_col, HD)]
             rows = start + lax.broadcasted_iota(jnp.int32, (1, CHUNK), 1)
             bias = jnp.where((rows >= lo) & (rows < hi), 0.0, -jnp.inf)
-            scores = lax.dot_general(
-                query, keys, (((1,), (1,)), ((), ())), preferred_element_type=jnp.float32
+            scores = jnp.dot(
+                query, keys_t[:, pl.ds(start, CHUNK)], preferred_element_type=jnp.float32
             ) * (HD ** (-0.5)) + bias
             new_peak = jnp.maximum(peak, jnp.max(scores, axis=1, keepdims=True))
             scale = jnp.exp(peak - new_peak)
@@ -257,6 +257,7 @@
                 pl.BlockSpec((group_size, C, 1), lambda b, j, lo, hi: (j, b, 0)),
                 pl.BlockSpec((group_size, C, 1), lambda b, j, lo, hi: (j, b, 0)),
             ],
+            scratch_shapes=[pltpu.VMEM((width, cache_rows.shape[0]), jnp.bfloat16)],
         ),
         compiler_params=pltpu.CompilerParams(vmem_limit_bytes=48 * 1024 * 1024),
     )(lo, hi, queries, cache_rows)

time: 212 us -> 202 us (0.953); the launches traced: 209 us -> 202 us
  waiting for transfers between devices: 19.4 us -> 8.12 us
  Pallas kernels: 121 us -> 128 us
  starting transfers between devices: 9.93 us -> 6.6 us
    pallas_call x1, Pallas kernels: 20.5 us -> 35.1 us  [cache_attention(): pl.pallas_call(attention_kernel, out_shape=(jax.ShapeDtypeStruct((heads,...]
    ppermute x4 -> x2, waiting for transfers between devices: 19.3 us -> 8.11 us  [branch(): return lambda t: jax.tree.map(lambda a: lax.ppermute(a, 'grp', pairs), t)]
    pallas_call x3, Pallas kernels: 71.2 us -> 62.7 us  [tp_exchange(): pl.pallas_call(functools.partial(exchange_kernel, count, stride, tuple(mo...]
    ppermute x4 -> x2, starting transfers between devices: 4.71 us -> 1.38 us  [branch(): return lambda t: jax.tree.map(lambda a: lax.ppermute(a, 'grp', pairs), t)]
  transfers between devices with their start and end apart: 7 -> 5, of which waited for: 4 -> 2; matrix products, arithmetic and copies ran while one was open for 17% -> 17% of each run, Pallas kernels for 51% -> 56%
where the time goes in v3:
time: 202 us
  Pallas kernels  128 us (63%)
  other arithmetic  18.8 us (9%)
  local copies, waits for them, and re-layouts  18.6 us (9%)
  matrix products  10.5 us (5%)
  between operations  10.5 us (5%)
  waiting for transfers between devices  8.12 us (4%)
  starting transfers between devices  6.6 us (3%)
    pallas_call x3, Pallas kernels, tp_exchange(): pl.pallas_call(functools.partial(exchange_kernel, count, stride, tuple(mo...  62.7 us
    pallas_call x1, Pallas kernels, cache_attention(): pl.pallas_call(attention_kernel, out_shape=(jax.ShapeDtypeStruct((heads,...  35.1 us
    pallas_call x1, Pallas kernels, group_gather(): pl.pallas_call(functools.partial(gather_kernel, count), out_shape=tuple(s...  30.5 us
    unnamed x57, local copies, waits for them, and re-layouts  10.8 us
    ppermute x2, waiting for transfers between devices, branch(): return lambda t: jax.tree.map(lambda a: lax.ppermute(a, 'grp', pairs), t)  8.11 us
    pallas_call x2, other arithmetic, cache_attention(): pl.pallas_call(attention_kernel, out_shape=(jax.ShapeDtypeStruct((heads,...  5.54 us
    ppermute x3, starting transfers between devices, on_device(): w_received.append(lax.ppermute(send, 'tp', pairs))  5.22 us
    dot_general x4, matrix products, on_device(): jnp.dot(lax.dynamic_index_in_dim(attention_ring, source, 0, False), w_rec...  4.35 us
  transfers between devices with their start and end apart: 5, of which 2 were waited for; matrix products, arithmetic and copies ran while one was open for 17% of the time, Pallas kernels for 56%

profile of v3, /device:TPU:4, one launch (start us, length us, event | category | flops | bytes accessed | tf_op | source)
XLA Modules:
  0.0 201.7 jit_solution(7912797814117127887)
XLA Ops:
  0.0 2.6 %constant_dynamic-slice_fusion.3 = (bf16[256,512]{1,0:T(8,128)(2,1)S(1)}, bf16[256,512]{1,0:T(8,128)(2,1)S(1)}, bf16[256,512]{1,0:T(8,128)(2,1)S(1)}, bf16[256,5...) fusion(bf16[256,4096]{1,0:T(8,128)(2,1)} %param.36, ...), kind=kLoop, calls=%fused_computation.64 | loop fusion | bytes 4194336 | tf_op jit(solution)/shard_map/dynamic_slice | solution.py:305
  3.5 1.6 collective-permute-start.20
  5.9 1.7 collective-permute-start.22
  8.5 2.0 collective-permute-start.21
  21.1 2.2 %fusion = f32[256]{0:T(256)S(1)} fusion(bf16[256,4096]{1,0:T(8,128)(2,1)} %param.32), kind=kLoop, calls=%fused_computation.2 | loop fusion | flops 3145472 | bytes 2098176 | tf_op jit(solution)/shard_map/reduce_sum | solution.py:318
  23.4 1.2 fusion.9
  26.2 4.4 %conditional.4 = (bf16[2,128,128]{2,1,0:T(8,128)(2,1)S(1)}) conditional(s32[]{:T(128)} %clamp.11, bf16[2,128,128]{2,1,0:T(8,128)(2,1)S(1)} %slice.133, bf16[2,128,128]{2,1,0:T(8,128)(2,1)S(1)} %slice.133, bf16[2,128,128]{2,1,0:T(8,128)(2,1)S(1)} %slice.133, bf16[2,128,128]{2,1,0:T(8,128)(2,1)S(1)} %slice.133, ...), branch_computations={%region_1.2_spmd, %region_2.3_spmd, %region_3.4_spmd, %region_4.5_... | conditional | bytes 393264 | solution.py:284
  26.3 1.3 collective-permute-start.1
  27.5 3.1 %collective-permute-done.1 = bf16[2,128,128]{2,1,0:T(8,128)(2,1)S(1)} collective-permute-done((bf16[2,128,128]{2,1,0:T(8,128)(2,1)S(1)}, bf16[2,128,128]{2,1,0:T(8,128)(2,1)S(1)}, u32[]{:S(2)}, u32[]{:S(2)}) %collective-permute-start.1) | collective-permute-done | bytes 65568 | tf_op jit(solution)/shard_map/cond/branch_2_fun/ppermute | solution.py:279
  31.3 2.6 %convolution_convert_fusion = bf16[256,64]{0,1:T(8,128)(2,1)S(1)} fusion(bf16[4096,64]{0,1:T(8,128)(2,1)} %param.35, bf16[256,4096]{1,0:T(8,128)(2,1)} %param.32, f32[4096]{0:T(1024)S(1)} %copy-done.23, f32[256]{0:T(256)S(1)} %add_rsqrt_fusion), kind=kOutput, calls=%fused_computation.15 | convolution fusion | flops 138428416 | bytes 2671616 | tf_op jit(solution)/shard_map/dot_general | solution.py:324
  35.7 30.5 %shard_map.82 = (bf16[4,2,2,384,128]{4,3,2,1,0:T(8,128)(2,1)S(1)}, bf16[4,2,256,64]{3,2,1,0:T(8,128)(2,1)S(1)}) custom-call(bf16[2,384,128]{2,1,0:T(8,128)(2,1)S(1)} %copy-done.6, bf16[256,64]{1,0:T(8,128)(2,1)S(1)} %copy.80.refs_1_), custom_call_target="tpu_custom_call" | custom-call | tf_op jit(solution)/shard_map/pallas_call | solution.py:171
  66.2 1.2 copy-done.2
  69.0 1.4 copy-done.3
  70.4 35.1 %shard_map.83 = (f32[16,384,128]{2,1,0:T(8,128)S(1)}, f32[16,384,1]{2,1,0:T(8,128)}, f32[16,384,1]{2,1,0:T(8,128)}) custom-call(s32[3]{0:T(128)S(1)} %get-tuple-element.118.lo_ref, s32[3]{0:T(128)S(1)} %get-tuple-element.119.hi_ref, bf16[16,384,128]{2,1,0:T(8,128)(2,1)S(1)} %bitcast.67, bf16[1280,512]{1,0:T(8,128)(2,1)S(1)} %copy-done.5), custom_call_target="tpu_custom_call" | custom-call | tf_op jit(solution)/shard_map/pallas_call | solution.py:241
  105.4 1.5 convert_element_type.50
  106.9 2.8 %reduce = f32[16,384]{1,0:T(8,128)S(1)} reduce(f32[16,384,1]{2,1,0:T(8,128)} %get-tuple-element.67, f32[]{:T(128)} %constant.178), dimensions={2}, to_apply=%get-tuple-element.67.reduce_sub_computation | reduce | bytes 49156 | tf_op jit(solution)/shard_map/pallas_call | solution.py:241
  109.7 2.8 %reduce.1 = f32[16,384]{1,0:T(8,128)S(1)} reduce(f32[16,384,1]{2,1,0:T(8,128)} %get-tuple-element.68, f32[]{:T(128)} %constant.178), dimensions={2}, to_apply=%get-tuple-element.68.reduce_sub_computation | reduce | bytes 49156 | tf_op jit(solution)/shard_map/pallas_call | solution.py:241
  112.5 1.4 copy-done.1
  113.9 38.0 %shard_map.84 = (bf16[8,2,384,128]{3,2,1,0:T(8,128)(2,1)S(1)}, f32[8,2,384]{2,1,0:T(2,128)S(1)}, f32[8,2,384]{2,1,0:T(2,128)S(1)}) custom-call(bf16[8,2,384,128]{3,2,1,0:T(8,128)(2,1)S(1)} %bitcast.66, f32[8,2,384]{2,1,0:T(2,128)S(1)} %reshape.299.refs_1_, f32[8,2,384]{2,1,0:T(2,128)S(1)} %reshape.300.refs_2_), custom_call_target="tpu_custom_call" | custom-call | tf_op jit(solution)/shard_map/pallas_call | solution.py:89
  152.0 1.2 copy-done.4
  153.8 2.1 %multiply_reduce_fusion = f32[2,384,128]{2,1,0:T(8,128)S(1)} fusion(bf16[8,2,384,128]{3,2,1,0:T(8,128)(2,1)} %copy-done.4, f32[8,2,384]{2,1,0:T(2,128)S(1)} %get-tuple-element.81), kind=kLoop, calls=%fused_computation.5 | loop fusion | flops 2260992 | bytes 1990656 | tf_op jit(solution)/shard_map/reduce_sum | solution.py:358
  156.7 5.2 %conditional.6 = (f32[2,130,128]{2,1,0:T(8,128)S(1)}) conditional(s32[]{:T(128)} %clamp.11, f32[2,130,128]{2,1,0:T(8,128)S(1)} %pad_maximum_fusion.4, f32[2,130,128]{2,1,0:T(8,128)S(1)} %pad_maximum_fusion.4, f32[2,130,128]{2,1,0:T(8,128)S(1)} %pad_maximum_fusion.4, ...), branch_computations={%region_16.17_spmd, %region_17.18_spmd, %region_18.19_spmd, %regio... | conditional | bytes 798768 | solution.py:284
  156.8 5.0 %collective-permute-done.11 = f32[2,130,128]{2,1,0:T(8,128)S(1)} collective-permute-done((f32[2,130,128]{2,1,0:T(8,128)S(1)}, f32[2,130,128]{2,1,0:T(8,128)S(1)}, u32[]{:S(2)}, u32[]{:S(2)}) %collective-permute-start.11) | collective-permute-done | bytes 133152 | tf_op jit(solution)/shard_map/cond/branch_2_fun/ppermute | solution.py:279
  164.1 1.0 copy.96
  165.1 1.6 copy.99
  168.3 1.2 fusion.60
  170.4 1.2 fusion.7
  171.7 8.6 %shard_map.85 = bf16[4,256,256]{2,1,0:T(8,128)(2,1)S(1)} custom-call(bf16[256,256]{1,0:T(8,128)(2,1)S(1)} %copy.93.refs_0_), custom_call_target="tpu_custom_call" | custom-call | tf_op jit(solution)/shard_map/pallas_call | solution.py:89
  180.7 1.3 fusion.20
  182.0 1.3 convolution_add_fusion.1
  183.4 1.4 fusion.3
  184.8 16.1 %shard_map.86 = bf16[2,256,512]{2,1,0:T(8,128)(2,1)S(1)} custom-call(bf16[256,512]{1,0:T(8,128)(2,1)S(1)} %slice.161.refs_0_), custom_call_target="tpu_custom_call" | custom-call | tf_op jit(solution)/shard_map/pallas_call | solution.py:89
  (101 shorter events, 16.2 us)
Async XLA Ops:
  0.0 23.4 %copy-start = (bf16[4096,256]{1,0:T(8,128)(2,1)S(1)}, bf16[4096,256]{1,0:T(8,128)(2,1)}, u32[]{:S(2)}) copy-start(bf16[4096,256]{1,0:T(8,128)(2,1)} %param.34) | copy-start | bytes 6291460
  2.6 7.9 %copy-start.22 = (s32[32]{0:T(128)S(1)}, s32[32]{0:T(128)}, u32[]{:S(2)}) copy-start(s32[32]{0:T(128)} %param.39) | copy-start | bytes 388
  2.6 11.7 %copy-start.24 = (s32[64]{0:T(128)S(1)}, s32[64]{0:T(128)}, u32[]{:S(2)}) copy-start(s32[64]{0:T(128)} %param.38) | copy-start | bytes 772
  3.5 178.5 %collective-permute-start.20 = (bf16[256,1024]{1,0:T(8,128)(2,1)}, bf16[256,1024]{1,0:T(8,128)(2,1)}, u32[]{:S(2)}, u32[]{:S(2)}) collective-permute-start(bf16[256,1024]{1,0:T(8,128)(2,1)} %pad_maximum_fusion), channel_id=1, source_target_pairs={{0,2},{1,3},{2,4},{3,5},{4,6},{5,7},{6,0},{7,1},{8,10},{9,11},{10,... | collective-permute-start | bytes 1572872 | tf_op jit(solution)/shard_map/ppermute | solution.py:313
  5.1 18.3 %copy-start.23 = (f32[4096]{0:T(1024)S(1)}, f32[4096]{0:T(1024)}, u32[]{:S(2)}) copy-start(f32[4096]{0:T(1024)} %param.33) | copy-start | bytes 49156
  5.9 174.7 %collective-permute-start.22 = (bf16[256,1024]{1,0:T(8,128)(2,1)}, bf16[256,1024]{1,0:T(8,128)(2,1)}, u32[]{:S(2)}, u32[]{:S(2)}) collective-permute-start(bf16[256,1024]{1,0:T(8,128)(2,1)} %pad_maximum_fusion.2), channel_id=1, source_target_pairs={{0,6},{1,7},{2,0},{3,1},{4,2},{5,3},{6,4},{7,5},{8,14},{9,15},{10,... | collective-permute-start | bytes 1572872 | tf_op jit(solution)/shard_map/ppermute | solution.py:313
  8.5 174.9 %collective-permute-start.21 = (bf16[256,1024]{1,0:T(8,128)(2,1)}, bf16[256,1024]{1,0:T(8,128)(2,1)}, u32[]{:S(2)}, u32[]{:S(2)}) collective-permute-start(bf16[256,1024]{1,0:T(8,128)(2,1)} %pad_maximum_fusion.1), channel_id=1, source_target_pairs={{0,4},{1,5},{2,6},{3,7},{4,0},{5,1},{6,2},{7,3},{8,12},{9,13},{10,... | collective-permute-start | bytes 1572872 | tf_op jit(solution)/shard_map/ppermute | solution.py:313
  21.1 2.3 %copy-start.9 = (bf16[256,4096]{1,0:T(8,128)(2,1)S(1)}, bf16[256,4096]{1,0:T(8,128)(2,1)}, u32[]{:S(2)}) copy-start(bf16[256,4096]{1,0:T(8,128)(2,1)} %param.32) | copy-start | bytes 6291460
  25.4 0.7 copy-start.12
  25.4 0.7 copy-start.14
  26.2 4.4 %copy-start.10 = (bf16[2,256,128]{2,1,0:T(8,128)(2,1)}, bf16[2,256,128]{2,1,0:T(8,128)(2,1)S(1)}, u32[]{:S(2)}) copy-start(bf16[2,256,128]{2,1,0:T(8,128)(2,1)S(1)} %maximum_bitcast_fusion) | copy-start | bytes 393220
  26.3 4.4 %collective-permute-start.1 = (bf16[2,128,128]{2,1,0:T(8,128)(2,1)S(1)}, bf16[2,128,128]{2,1,0:T(8,128)(2,1)S(1)}, u32[]{:S(2)}, u32[]{:S(2)}) collective-permute-start(bf16[2,128,128]{2,1,0:T(8,128)(2,1)S(1)} %param.2), channel_id=1, source_target_pairs={{0,16},{8,24},{16,0},{24,8},{32,48},{40,56},{48,32},{56,40},{64,80... | collective-permute-start | bytes 196616 | tf_op jit(solution)/shard_map/cond/branch_2_fun/ppermute | solution.py:279
  31.3 37.7 %copy-start.5 = (bf16[1280,512]{1,0:T(8,128)(2,1)S(1)}, bf16[1280,512]{1,0:T(8,128)(2,1)}, u32[]{:S(2)}) copy-start(bf16[1280,512]{1,0:T(8,128)(2,1)} %cache_ref.1) | copy-start | bytes 3932164
  34.8 0.9 copy-start.6
  66.2 1.2 copy-start.2
  67.4 0.8 copy-start.7
  69.0 1.4 copy-start.3
  112.5 1.4 copy-start.1
  152.0 1.2 copy-start.4
  155.9 6.9 %copy-start.8 = (bf16[4,2,256,64]{3,2,1,0:T(8,128)(2,1)S(1)}, bf16[4,2,256,64]{3,2,1,0:T(8,128)(2,1)}, u32[]{:S(2)}) copy-start(bf16[4,2,256,64]{3,2,1,0:T(8,128)(2,1)} %copy-done.7) | copy-start | bytes 786436
  156.7 5.1 %collective-permute-start.11 = (f32[2,130,128]{2,1,0:T(8,128)S(1)}, f32[2,130,128]{2,1,0:T(8,128)S(1)}, u32[]{:S(2)}, u32[]{:S(2)}) collective-permute-start(f32[2,130,128]{2,1,0:T(8,128)S(1)} %param.14), channel_id=1, source_target_pairs={{0,16},{8,24},{16,0},{24,8},{32,48},{40,56},{48,32},{56,40},{64,80... | collective-permute-start | bytes 399368 | tf_op jit(solution)/shard_map/cond/branch_2_fun/ppermute | solution.py:279
  161.9 5.4 %copy-start.13 = (f32[256,64]{1,0:T(8,128)S(1)}, f32[256,64]{1,0:T(8,128)}, u32[]{:S(2)}) copy-start(f32[256,64]{1,0:T(8,128)} %copy-done.12) | copy-start | bytes 196612
  161.9 5.4 %copy-start.15 = (f32[256,64]{1,0:T(8,128)S(1)}, f32[256,64]{1,0:T(8,128)}, u32[]{:S(2)}) copy-start(f32[256,64]{1,0:T(8,128)} %copy-done.14) | copy-start | bytes 196612
  162.8 5.5 %copy-start.11 = (bf16[2,256,128]{2,1,0:T(8,128)(2,1)S(1)}, bf16[2,256,128]{2,1,0:T(8,128)(2,1)}, u32[]{:S(2)}) copy-start(bf16[2,256,128]{2,1,0:T(8,128)(2,1)} %copy-done.10) | copy-start | bytes 393220
  163.7 3.0 %copy-start.20 = (f32[2,1,128]{2,1,0:T(1,128)S(1)}, f32[2,1,128]{2,1,0:T(1,128)}, u32[]{:S(2)}) copy-start(f32[2,1,128]{2,1,0:T(1,128)} %get-tuple-element.101) | copy-start | bytes 3076
  163.7 3.0 %copy-start.21 = (f32[2,1,128]{2,1,0:T(1,128)S(1)}, f32[2,1,128]{2,1,0:T(1,128)}, u32[]{:S(2)}) copy-start(f32[2,1,128]{2,1,0:T(1,128)} %get-tuple-element.102) | copy-start | bytes 3076
  167.3 2.3 %copy-start.18 = (f32[2,128]{1,0:T(2,128)S(1)}, f32[2,128]{1,0:T(2,128)}, u32[]{:S(2)}) copy-start(f32[2,128]{1,0:T(2,128)} %get-tuple-element.77) | copy-start | bytes 3076
  167.4 2.3 %copy-start.19 = (f32[2,128]{1,0:T(2,128)S(1)}, f32[2,128]{1,0:T(2,128)}, u32[]{:S(2)}) copy-start(f32[2,128]{1,0:T(2,128)} %get-tuple-element.78) | copy-start | bytes 3076
  168.3 12.1 %copy-start.16 = (bf16[256,512]{1,0:T(8,128)(2,1)S(1)}, bf16[256,512]{1,0:T(8,128)(2,1)}, u32[]{:S(2)}) copy-start(bf16[256,512]{1,0:T(8,128)(2,1)} %get-tuple-element.86) | copy-start | bytes 786436
  168.3 12.1 %copy-start.17 = (bf16[256,512]{1,0:T(8,128)(2,1)S(1)}, bf16[256,512]{1,0:T(8,128)(2,1)}, u32[]{:S(2)}) copy-start(bf16[256,512]{1,0:T(8,128)(2,1)} %get-tuple-element.87) | copy-start | bytes 786436

commit v4 on v2

--- a/solution.py
+++ b/solution.py
@@ -16,7 +16,7 @@
 THETA = 5000000.0
 EPS = 1e-05
 NEG = -1e30
-CHUNK = 640
+CHUNK = 1280
 MESH = pl.DeviceIdType.MESH
 
 

time: 212 us -> 207 us (0.976); the launches traced: 209 us -> 209 us
  starting transfers between devices: 9.93 us -> 38.1 us
  Pallas kernels: 121 us -> 100 us
  waiting for transfers between devices: 19.4 us -> 11.4 us
    ppermute x4, starting transfers between devices: 4.71 us -> 32.8 us  [branch(): return lambda t: jax.tree.map(lambda a: lax.ppermute(a, 'grp', pairs), t)]
    pallas_call x3, Pallas kernels: 71.2 us -> 55.9 us  [tp_exchange(): pl.pallas_call(functools.partial(exchange_kernel, count, stride, tuple(mo...]
    ppermute x4, waiting for transfers between devices: 19.3 us -> 11.4 us  [branch(): return lambda t: jax.tree.map(lambda a: lax.ppermute(a, 'grp', pairs), t)]
    pallas_call x1, Pallas kernels: 20.5 us -> 14.9 us  [cache_attention(): pl.pallas_call(attention_kernel, out_shape=(jax.ShapeDtypeStruct((heads,...]
  transfers between devices with their start and end apart: 7 -> 7, of which waited for: 4 -> 4; matrix products, arithmetic and copies ran while one was open for 17% -> 17% of each run, Pallas kernels for 51% -> 41%
where the time goes in v4:
time: 207 us; the launch traced here: 209 us
  Pallas kernels  100 us (48%)
  starting transfers between devices  38.1 us (18%)
  other arithmetic  18.8 us (9%)
  local copies, waits for them, and re-layouts  18.6 us (9%)
  waiting for transfers between devices  11.4 us (6%)
  matrix products  10.5 us (5%)
  between operations  10.5 us (5%)
    pallas_call x3, Pallas kernels, tp_exchange(): pl.pallas_call(functools.partial(exchange_kernel, count, stride, tuple(mo...  55.9 us
    ppermute x4, starting transfers between devices, branch(): return lambda t: jax.tree.map(lambda a: lax.ppermute(a, 'grp', pairs), t)  32.8 us
    pallas_call x1, Pallas kernels, group_gather(): pl.pallas_call(functools.partial(gather_kernel, count), out_shape=tuple(s...  29.7 us
    pallas_call x1, Pallas kernels, cache_attention(): pl.pallas_call(attention_kernel, out_shape=(jax.ShapeDtypeStruct((heads,...  14.9 us
    ppermute x4, waiting for transfers between devices, branch(): return lambda t: jax.tree.map(lambda a: lax.ppermute(a, 'grp', pairs), t)  11.4 us
    unnamed x57, local copies, waits for them, and re-layouts  10.8 us
    pallas_call x2, other arithmetic, cache_attention(): pl.pallas_call(attention_kernel, out_shape=(jax.ShapeDtypeStruct((heads,...  5.54 us
    ppermute x3, starting transfers between devices, on_device(): w_received.append(lax.ppermute(send, 'tp', pairs))  5.22 us
  transfers between devices with their start and end apart: 7, of which 4 were waited for; matrix products, arithmetic and copies ran while one was open for 17% of the time, Pallas kernels for 41%

profile of v4, /device:TPU:4, one launch (start us, length us, event | category | flops | bytes accessed | tf_op | source)
XLA Modules:
  0.0 208.6 jit_solution(5408992414914876902)
XLA Ops:
  0.0 2.6 %constant_dynamic-slice_fusion.3 = (bf16[256,512]{1,0:T(8,128)(2,1)S(1)}, bf16[256,512]{1,0:T(8,128)(2,1)S(1)}, bf16[256,512]{1,0:T(8,128)(2,1)S(1)}, bf16[256,5...) fusion(bf16[256,4096]{1,0:T(8,128)(2,1)} %param.36, ...), kind=kLoop, calls=%fused_computation.64 | loop fusion | bytes 4194336 | tf_op jit(solution)/shard_map/dynamic_slice | solution.py:304
  3.5 1.6 collective-permute-start.20
  5.9 1.7 collective-permute-start.22
  8.5 2.0 collective-permute-start.21
  21.1 2.2 %fusion = f32[256]{0:T(256)S(1)} fusion(bf16[256,4096]{1,0:T(8,128)(2,1)} %param.32), kind=kLoop, calls=%fused_computation.2 | loop fusion | flops 3145472 | bytes 2098176 | tf_op jit(solution)/shard_map/reduce_sum | solution.py:317
  26.2 4.4 %conditional.4 = (bf16[2,128,128]{2,1,0:T(8,128)(2,1)S(1)}) conditional(s32[]{:T(128)} %clamp.11, bf16[2,128,128]{2,1,0:T(8,128)(2,1)S(1)} %slice.133, bf16[2,128,128]{2,1,0:T(8,128)(2,1)S(1)} %slice.133, bf16[2,128,128]{2,1,0:T(8,128)(2,1)S(1)} %slice.133, bf16[2,128,128]{2,1,0:T(8,128)(2,1)S(1)} %slice.133, ...), branch_computations={%region_1.2_spmd, %region_2.3_spmd, %region_3.4_spmd, %region_4.5_... | conditional | bytes 393264 | solution.py:283
  27.5 3.1 %collective-permute-done.1 = bf16[2,128,128]{2,1,0:T(8,128)(2,1)S(1)} collective-permute-done((bf16[2,128,128]{2,1,0:T(8,128)(2,1)S(1)}, bf16[2,128,128]{2,1,0:T(8,128)(2,1)S(1)}, u32[]{:S(2)}, u32[]{:S(2)}) %collective-permute-start.1) | collective-permute-done | bytes 65568 | tf_op jit(solution)/shard_map/cond/branch_2_fun/ppermute | solution.py:278
  30.6 5.5 %conditional.5 = (bf16[2,128,128]{2,1,0:T(8,128)(2,1)S(1)}) conditional(s32[]{:T(128)} %clamp.10, bf16[2,128,128]{2,1,0:T(8,128)(2,1)S(1)} %get-tuple-element.120, bf16[2,128,128]{2,1,0:T(8,128)(2,1)S(1)} %get-tuple-element.120, bf16[2,128,128]{2,1,0:T(8,128)(2,1)S(1)} %get-tuple-element.120, ...), branch_computations={%region_9.10_spmd, %region_10.11_spmd, %region_11.12_spmd, %region... | conditional | bytes 393264 | solution.py:285
  30.6 3.3 %collective-permute-start.8 = (bf16[2,128,128]{2,1,0:T(8,128)(2,1)S(1)}, bf16[2,128,128]{2,1,0:T(8,128)(2,1)S(1)}, u32[]{:S(2)}, u32[]{:S(2)}) collective-permute-start(bf16[2,128,128]{2,1,0:T(8,128)(2,1)S(1)} %param.10), channel_id=1, source_target_pairs={{0,128},{8,136},{16,144},{24,152},{32,160},{40,168},{48,176},{56,1... | collective-permute-start | bytes 196616 | tf_op jit(solution)/shard_map/cond/branch_2_fun/ppermute | solution.py:278
  33.9 2.2 %collective-permute-done.8 = bf16[2,128,128]{2,1,0:T(8,128)(2,1)S(1)} collective-permute-done((bf16[2,128,128]{2,1,0:T(8,128)(2,1)S(1)}, bf16[2,128,128]{2,1,0:T(8,128)(2,1)S(1)}, u32[]{:S(2)}, u32[]{:S(2)}) %collective-permute-start.8) | collective-permute-done | bytes 65568 | tf_op jit(solution)/shard_map/cond/branch_2_fun/ppermute | solution.py:278
  36.8 2.6 %convolution_convert_fusion = bf16[256,64]{0,1:T(8,128)(2,1)S(1)} fusion(bf16[4096,64]{0,1:T(8,128)(2,1)} %param.35, bf16[256,4096]{1,0:T(8,128)(2,1)} %param.32, f32[4096]{0:T(1024)S(1)} %copy-done.23, f32[256]{0:T(256)S(1)} %add_rsqrt_fusion), kind=kOutput, calls=%fused_computation.15 | convolution fusion | flops 138428416 | bytes 2671616 | tf_op jit(solution)/shard_map/dot_general | solution.py:323
  41.2 29.7 %shard_map.82 = (bf16[4,2,2,384,128]{4,3,2,1,0:T(8,128)(2,1)S(1)}, bf16[4,2,256,64]{3,2,1,0:T(8,128)(2,1)S(1)}) custom-call(bf16[2,384,128]{2,1,0:T(8,128)(2,1)S(1)} %copy-done.6, bf16[256,64]{1,0:T(8,128)(2,1)S(1)} %copy.80.refs_1_), custom_call_target="tpu_custom_call" | custom-call | tf_op jit(solution)/shard_map/pallas_call | solution.py:171
  73.7 1.4 copy-done.3
  75.1 14.9 %shard_map.83 = (f32[16,384,128]{2,1,0:T(8,128)S(1)}, f32[16,384,1]{2,1,0:T(8,128)}, f32[16,384,1]{2,1,0:T(8,128)}) custom-call(s32[3]{0:T(128)S(1)} %get-tuple-element.118.lo_ref, s32[3]{0:T(128)S(1)} %get-tuple-element.119.hi_ref, bf16[16,384,128]{2,1,0:T(8,128)(2,1)S(1)} %bitcast.67, bf16[1280,512]{1,0:T(8,128)(2,1)S(1)} %copy-done.5), custom_call_target="tpu_custom_call" | custom-call | tf_op jit(solution)/shard_map/pallas_call | solution.py:241
  90.0 1.5 convert_element_type.50
  91.5 2.8 %reduce = f32[16,384]{1,0:T(8,128)S(1)} reduce(f32[16,384,1]{2,1,0:T(8,128)} %get-tuple-element.67, f32[]{:T(128)} %constant.178), dimensions={2}, to_apply=%get-tuple-element.67.reduce_sub_computation | reduce | bytes 49156 | tf_op jit(solution)/shard_map/pallas_call | solution.py:241
  94.3 2.8 %reduce.1 = f32[16,384]{1,0:T(8,128)S(1)} reduce(f32[16,384,1]{2,1,0:T(8,128)} %get-tuple-element.68, f32[]{:T(128)} %constant.178), dimensions={2}, to_apply=%get-tuple-element.68.reduce_sub_computation | reduce | bytes 49156 | tf_op jit(solution)/shard_map/pallas_call | solution.py:241
  97.1 1.4 copy-done.1
  98.5 32.3 %shard_map.84 = (bf16[8,2,384,128]{3,2,1,0:T(8,128)(2,1)S(1)}, f32[8,2,384]{2,1,0:T(2,128)S(1)}, f32[8,2,384]{2,1,0:T(2,128)S(1)}) custom-call(bf16[8,2,384,128]{3,2,1,0:T(8,128)(2,1)S(1)} %bitcast.66, f32[8,2,384]{2,1,0:T(2,128)S(1)} %reshape.299.refs_1_, f32[8,2,384]{2,1,0:T(2,128)S(1)} %reshape.300.refs_2_), custom_call_target="tpu_custom_call" | custom-call | tf_op jit(solution)/shard_map/pallas_call | solution.py:89
  132.7 2.1 %multiply_reduce_fusion = f32[2,384,128]{2,1,0:T(8,128)S(1)} fusion(bf16[8,2,384,128]{3,2,1,0:T(8,128)(2,1)} %copy-done.4, f32[8,2,384]{2,1,0:T(2,128)S(1)} %get-tuple-element.81), kind=kLoop, calls=%fused_computation.5 | loop fusion | flops 2260992 | bytes 1990656 | tf_op jit(solution)/shard_map/reduce_sum | solution.py:357
  135.6 14.9 %conditional.6 = (f32[2,130,128]{2,1,0:T(8,128)S(1)}) conditional(s32[]{:T(128)} %clamp.11, f32[2,130,128]{2,1,0:T(8,128)S(1)} %pad_maximum_fusion.4, f32[2,130,128]{2,1,0:T(8,128)S(1)} %pad_maximum_fusion.4, f32[2,130,128]{2,1,0:T(8,128)S(1)} %pad_maximum_fusion.4, ...), branch_computations={%region_16.17_spmd, %region_17.18_spmd, %region_18.19_spmd, %regio... | conditional | bytes 798768 | solution.py:283
  135.6 11.9 %collective-permute-start.11 = (f32[2,130,128]{2,1,0:T(8,128)S(1)}, f32[2,130,128]{2,1,0:T(8,128)S(1)}, u32[]{:S(2)}, u32[]{:S(2)}) collective-permute-start(f32[2,130,128]{2,1,0:T(8,128)S(1)} %param.14), channel_id=1, source_target_pairs={{0,16},{8,24},{16,0},{24,8},{32,48},{40,56},{48,32},{56,40},{64,80... | collective-permute-start | bytes 399368 | tf_op jit(solution)/shard_map/cond/branch_2_fun/ppermute | solution.py:278
  147.4 3.0 %collective-permute-done.11 = f32[2,130,128]{2,1,0:T(8,128)S(1)} collective-permute-done((f32[2,130,128]{2,1,0:T(8,128)S(1)}, f32[2,130,128]{2,1,0:T(8,128)S(1)}, u32[]{:S(2)}, u32[]{:S(2)}) %collective-permute-start.11) | collective-permute-done | bytes 133152 | tf_op jit(solution)/shard_map/cond/branch_2_fun/ppermute | solution.py:278
  150.5 19.7 %conditional.7 = (f32[2,130,128]{2,1,0:T(8,128)S(1)}) conditional(s32[]{:T(128)} %clamp.10, f32[2,130,128]{2,1,0:T(8,128)S(1)} %get-tuple-element.122, f32[2,130,128]{2,1,0:T(8,128)S(1)} %get-tuple-element.122, f32[2,130,128]{2,1,0:T(8,128)S(1)} %get-tuple-element.122, f32[2,130,128]{2,1,0:T(8,128)S(1)} %get-tuple-element.122), branch_computations={%region_24.25_spmd, %region_25.26_spmd, %region_26.27_spmd, %regio... | conditional | bytes 798768 | solution.py:285
  150.6 16.4 %collective-permute-start.18 = (f32[2,130,128]{2,1,0:T(8,128)S(1)}, f32[2,130,128]{2,1,0:T(8,128)S(1)}, u32[]{:S(2)}, u32[]{:S(2)}) collective-permute-start(f32[2,130,128]{2,1,0:T(8,128)S(1)} %param.22), channel_id=1, source_target_pairs={{0,128},{8,136},{16,144},{24,152},{32,160},{40,168},{48,176},{56,1... | collective-permute-start | bytes 399368 | tf_op jit(solution)/shard_map/cond/branch_2_fun/ppermute | solution.py:278
  167.0 3.0 %collective-permute-done.18 = f32[2,130,128]{2,1,0:T(8,128)S(1)} collective-permute-done((f32[2,130,128]{2,1,0:T(8,128)S(1)}, f32[2,130,128]{2,1,0:T(8,128)S(1)}, u32[]{:S(2)}, u32[]{:S(2)}) %collective-permute-start.18) | collective-permute-done | bytes 133152 | tf_op jit(solution)/shard_map/cond/branch_2_fun/ppermute | solution.py:278
  173.2 1.6 copy.99
  179.8 8.1 %shard_map.85 = bf16[4,256,256]{2,1,0:T(8,128)(2,1)S(1)} custom-call(bf16[256,256]{1,0:T(8,128)(2,1)S(1)} %copy.93.refs_0_), custom_call_target="tpu_custom_call" | custom-call | tf_op jit(solution)/shard_map/pallas_call | solution.py:89
  188.3 1.3 fusion.20
  189.6 1.3 convolution_add_fusion.1
  191.0 1.4 fusion.3
  192.4 15.4 %shard_map.86 = bf16[2,256,512]{2,1,0:T(8,128)(2,1)S(1)} custom-call(bf16[256,512]{1,0:T(8,128)(2,1)S(1)} %slice.161.refs_0_), custom_call_target="tpu_custom_call" | custom-call | tf_op jit(solution)/shard_map/pallas_call | solution.py:89
  (107 shorter events, 24.1 us)
Async XLA Ops:
  0.0 23.4 %copy-start = (bf16[4096,256]{1,0:T(8,128)(2,1)S(1)}, bf16[4096,256]{1,0:T(8,128)(2,1)}, u32[]{:S(2)}) copy-start(bf16[4096,256]{1,0:T(8,128)(2,1)} %param.34) | copy-start | bytes 6291460
  2.6 7.9 %copy-start.22 = (s32[32]{0:T(128)S(1)}, s32[32]{0:T(128)}, u32[]{:S(2)}) copy-start(s32[32]{0:T(128)} %param.39) | copy-start | bytes 388
  2.6 11.7 %copy-start.24 = (s32[64]{0:T(128)S(1)}, s32[64]{0:T(128)}, u32[]{:S(2)}) copy-start(s32[64]{0:T(128)} %param.38) | copy-start | bytes 772
  3.5 186.1 %collective-permute-start.20 = (bf16[256,1024]{1,0:T(8,128)(2,1)}, bf16[256,1024]{1,0:T(8,128)(2,1)}, u32[]{:S(2)}, u32[]{:S(2)}) collective-permute-start(bf16[256,1024]{1,0:T(8,128)(2,1)} %pad_maximum_fusion), channel_id=1, source_target_pairs={{0,2},{1,3},{2,4},{3,5},{4,6},{5,7},{6,0},{7,1},{8,10},{9,11},{10,... | collective-permute-start | bytes 1572872 | tf_op jit(solution)/shard_map/ppermute | solution.py:312
  5.1 18.3 %copy-start.23 = (f32[4096]{0:T(1024)S(1)}, f32[4096]{0:T(1024)}, u32[]{:S(2)}) copy-start(f32[4096]{0:T(1024)} %param.33) | copy-start | bytes 49156
  5.9 182.3 %collective-permute-start.22 = (bf16[256,1024]{1,0:T(8,128)(2,1)}, bf16[256,1024]{1,0:T(8,128)(2,1)}, u32[]{:S(2)}, u32[]{:S(2)}) collective-permute-start(bf16[256,1024]{1,0:T(8,128)(2,1)} %pad_maximum_fusion.2), channel_id=1, source_target_pairs={{0,6},{1,7},{2,0},{3,1},{4,2},{5,3},{6,4},{7,5},{8,14},{9,15},{10,... | collective-permute-start | bytes 1572872 | tf_op jit(solution)/shard_map/ppermute | solution.py:312
  8.5 182.5 %collective-permute-start.21 = (bf16[256,1024]{1,0:T(8,128)(2,1)}, bf16[256,1024]{1,0:T(8,128)(2,1)}, u32[]{:S(2)}, u32[]{:S(2)}) collective-permute-start(bf16[256,1024]{1,0:T(8,128)(2,1)} %pad_maximum_fusion.1), channel_id=1, source_target_pairs={{0,4},{1,5},{2,6},{3,7},{4,0},{5,1},{6,2},{7,3},{8,12},{9,13},{10,... | collective-permute-start | bytes 1572872 | tf_op jit(solution)/shard_map/ppermute | solution.py:312
  21.1 2.3 %copy-start.9 = (bf16[256,4096]{1,0:T(8,128)(2,1)S(1)}, bf16[256,4096]{1,0:T(8,128)(2,1)}, u32[]{:S(2)}) copy-start(bf16[256,4096]{1,0:T(8,128)(2,1)} %param.32) | copy-start | bytes 6291460
  25.4 0.7 copy-start.12
  25.4 0.7 copy-start.14
  26.2 9.9 %copy-start.10 = (bf16[2,256,128]{2,1,0:T(8,128)(2,1)}, bf16[2,256,128]{2,1,0:T(8,128)(2,1)S(1)}, u32[]{:S(2)}) copy-start(bf16[2,256,128]{2,1,0:T(8,128)(2,1)S(1)} %maximum_bitcast_fusion) | copy-start | bytes 393220
  26.3 4.4 %collective-permute-start.1 = (bf16[2,128,128]{2,1,0:T(8,128)(2,1)S(1)}, bf16[2,128,128]{2,1,0:T(8,128)(2,1)S(1)}, u32[]{:S(2)}, u32[]{:S(2)}) collective-permute-start(bf16[2,128,128]{2,1,0:T(8,128)(2,1)S(1)} %param.2), channel_id=1, source_target_pairs={{0,16},{8,24},{16,0},{24,8},{32,48},{40,56},{48,32},{56,40},{64,80... | collective-permute-start | bytes 196616 | tf_op jit(solution)/shard_map/cond/branch_2_fun/ppermute | solution.py:278
  30.6 5.5 %collective-permute-start.8 = (bf16[2,128,128]{2,1,0:T(8,128)(2,1)S(1)}, bf16[2,128,128]{2,1,0:T(8,128)(2,1)S(1)}, u32[]{:S(2)}, u32[]{:S(2)}) collective-permute-start(bf16[2,128,128]{2,1,0:T(8,128)(2,1)S(1)} %param.10), channel_id=1, source_target_pairs={{0,128},{8,136},{16,144},{24,152},{32,160},{40,168},{48,176},{56,1... | collective-permute-start | bytes 196616 | tf_op jit(solution)/shard_map/cond/branch_2_fun/ppermute | solution.py:278
  36.8 36.9 %copy-start.5 = (bf16[1280,512]{1,0:T(8,128)(2,1)S(1)}, bf16[1280,512]{1,0:T(8,128)(2,1)}, u32[]{:S(2)}) copy-start(bf16[1280,512]{1,0:T(8,128)(2,1)} %cache_ref.1) | copy-start | bytes 3932164
  40.3 0.9 copy-start.6
  70.9 1.2 copy-start.2
  72.1 0.8 copy-start.7
  73.7 1.4 copy-start.3
  97.1 1.4 copy-start.1
  130.8 1.2 copy-start.4
  134.8 36.1 %copy-start.8 = (bf16[4,2,256,64]{3,2,1,0:T(8,128)(2,1)S(1)}, bf16[4,2,256,64]{3,2,1,0:T(8,128)(2,1)}, u32[]{:S(2)}) copy-start(bf16[4,2,256,64]{3,2,1,0:T(8,128)(2,1)} %copy-done.7) | copy-start | bytes 786436
  135.6 14.9 %collective-permute-start.11 = (f32[2,130,128]{2,1,0:T(8,128)S(1)}, f32[2,130,128]{2,1,0:T(8,128)S(1)}, u32[]{:S(2)}, u32[]{:S(2)}) collective-permute-start(f32[2,130,128]{2,1,0:T(8,128)S(1)} %param.14), channel_id=1, source_target_pairs={{0,16},{8,24},{16,0},{24,8},{32,48},{40,56},{48,32},{56,40},{64,80... | collective-permute-start | bytes 399368 | tf_op jit(solution)/shard_map/cond/branch_2_fun/ppermute | solution.py:278
  150.5 24.9 %copy-start.13 = (f32[256,64]{1,0:T(8,128)S(1)}, f32[256,64]{1,0:T(8,128)}, u32[]{:S(2)}) copy-start(f32[256,64]{1,0:T(8,128)} %copy-done.12) | copy-start | bytes 196612
  150.5 24.9 %copy-start.15 = (f32[256,64]{1,0:T(8,128)S(1)}, f32[256,64]{1,0:T(8,128)}, u32[]{:S(2)}) copy-start(f32[256,64]{1,0:T(8,128)} %copy-done.14) | copy-start | bytes 196612
  150.6 19.5 %collective-permute-start.18 = (f32[2,130,128]{2,1,0:T(8,128)S(1)}, f32[2,130,128]{2,1,0:T(8,128)S(1)}, u32[]{:S(2)}, u32[]{:S(2)}) collective-permute-start(f32[2,130,128]{2,1,0:T(8,128)S(1)} %param.22), channel_id=1, source_target_pairs={{0,128},{8,136},{16,144},{24,152},{32,160},{40,168},{48,176},{56,1... | collective-permute-start | bytes 399368 | tf_op jit(solution)/shard_map/cond/branch_2_fun/ppermute | solution.py:278
  170.9 5.5 %copy-start.11 = (bf16[2,256,128]{2,1,0:T(8,128)(2,1)S(1)}, bf16[2,256,128]{2,1,0:T(8,128)(2,1)}, u32[]{:S(2)}) copy-start(bf16[2,256,128]{2,1,0:T(8,128)(2,1)} %copy-done.10) | copy-start | bytes 393220
  171.8 3.0 %copy-start.20 = (f32[2,1,128]{2,1,0:T(1,128)S(1)}, f32[2,1,128]{2,1,0:T(1,128)}, u32[]{:S(2)}) copy-start(f32[2,1,128]{2,1,0:T(1,128)} %get-tuple-element.101) | copy-start | bytes 3076
  171.8 3.0 %copy-start.21 = (f32[2,1,128]{2,1,0:T(1,128)S(1)}, f32[2,1,128]{2,1,0:T(1,128)}, u32[]{:S(2)}) copy-start(f32[2,1,128]{2,1,0:T(1,128)} %get-tuple-element.102) | copy-start | bytes 3076
  175.4 2.3 %copy-start.18 = (f32[2,128]{1,0:T(2,128)S(1)}, f32[2,128]{1,0:T(2,128)}, u32[]{:S(2)}) copy-start(f32[2,128]{1,0:T(2,128)} %get-tuple-element.77) | copy-start | bytes 3076
  175.4 2.3 %copy-start.19 = (f32[2,128]{1,0:T(2,128)S(1)}, f32[2,128]{1,0:T(2,128)}, u32[]{:S(2)}) copy-start(f32[2,128]{1,0:T(2,128)} %get-tuple-element.78) | copy-start | bytes 3076
  176.4 11.6 %copy-start.16 = (bf16[256,512]{1,0:T(8,128)(2,1)S(1)}, bf16[256,512]{1,0:T(8,128)(2,1)}, u32[]{:S(2)}) copy-start(bf16[256,512]{1,0:T(8,128)(2,1)} %get-tuple-element.86) | copy-start | bytes 786436
  176.4 11.6 %copy-start.17 = (bf16[256,512]{1,0:T(8,128)(2,1)S(1)}, bf16[256,512]{1,0:T(8,128)(2,1)}, u32[]{:S(2)}) copy-start(bf16[256,512]{1,0:T(8,128)(2,1)} %get-tuple-element.87) | copy-start | bytes 786436
